TPU v7x, 32 devices: a whole 2x2x4 slice. The times are simulated.
32 devices in a mesh: parts: 2 (over y), col: 16 (over z, x, core).
Axes of the slice: x: 2, y: 2, z: 4, core: 2. Of those that a mesh axis runs over, the one named last changes fastest.
Arguments:
- alignment_rows: bfloat16 [128, 128, 256], P('parts', 'col'), parts along dimension 0, may hold values from -6 to 6
- alignment_columns: bfloat16 [128, 256, 256], P('parts', 'col'), parts along dimension 0, may hold values from -6 to 6
- slab_alignment_mask: int32 [128, 128], P('parts'), parts along dimension 0, may hold values 0 or 1
- slab_crop_mask: int32 [256], P('parts'), parts along dimension 0, may hold values 0 or 1
- column_alignment_mask: int32 [128, 256], P('parts', 'col'), parts along dimension 0, may hold values 0 or 1
- column_crop_mask: int32 [512], P(('parts', 'col')), parts along dimension 0, may hold values 0 or 1
- norm_scale_gain: float32 [256], replicated, may hold values from 0.25 to 1.75
- norm_offset_bias: float32 [256], replicated, may hold values from -3 to 3
- left_projection_weight: bfloat16 [256, 32], replicated, may hold values from -0.375 to 0.375
- right_projection_weight: bfloat16 [256, 32], replicated, may hold values from -0.375 to 0.375
- pair_output_weight: bfloat16 [1024, 128], replicated, may hold values from -1.5 to 1.5
- pair_output_bias: float32 [128], replicated, may hold values from -3 to 3
- pair_update_gradient: bfloat16 [256, 256, 128], P('parts', 'col'), parts along dimension 0, may hold values from -4 to 4
Outputs:
- pair_out: bfloat16 [256, 256, 128], P('parts', 'col'), parts along dimension 0
- grad_rows: bfloat16 [128, 128, 256], P('parts', 'col'), parts along dimension 0
- grad_cols: bfloat16 [128, 256, 256], P('parts', 'col'), parts along dimension 0
- grad_pair_weight: float32 [2048, 128], P(('parts', 'col')), parts along dimension 0
- grad_proj: float32 [512, 64], P(('parts', 'col')), parts along dimension 0
There are 2 independent parts, one for each index of `parts`. A program takes and returns all parts, laid end to end along the dimension named above; an argument that names none is the same for every part. Nothing has to cross between parts.
All inputs are finite; a program needn't handle non-finite values. No bound on the sum of `column_alignment_mask` or of `column_crop_mask` on one device may be relied on, other than what follows from the above.
Results may differ from a plain program's by a relative error of at most 0.007.
Values may be sent and summed in bfloat16 or wider, within the bound.
A program may use at most 128 MiB of HBM per device.

v0:
```python
import jax
import jax.numpy as jnp
from jax import lax
from jax.sharding import PartitionSpec as P

ALIGNMENT_WIDTH = 256
PROJECTED_WIDTH = 32
PAIR_WIDTH = 128
ALIGNMENT_COUNT = 64
SLAB_ROW_COUNT = 128
COLUMN_RESIDUES = 16


norm_eps = 1e-05
row_block_inputs = 64


def apply_layer_norm(value_array, gain, shift):
    value_array = value_array.astype(jnp.float32)
    center = value_array - jnp.mean(value_array, axis=-1, keepdims=True)
    spread = jnp.mean(center * center, axis=-1, keepdims=True)
    return center * lax.rsqrt(spread + norm_eps) * gain + shift


def per_device(
    alignment_rows,
    alignment_columns,
    slab_alignment_mask,
    slab_crop_mask,
    column_alignment_mask,
    column_crop_mask,
    norm_scale_gain,
    norm_offset_bias,
    left_projection_weight,
    right_projection_weight,
    pair_output_weight,
    pair_output_bias,
    pair_update_gradient,
):
    local_rows = alignment_rows.shape[1]
    position = lax.axis_index("col")
    row_mask_weight = (slab_alignment_mask * slab_crop_mask[None, :]).astype(jnp.float32)
    local_mask_weight = lax.dynamic_slice_in_dim(
        row_mask_weight, position * local_rows, local_rows, 1
    )
    column_mask_weight = (column_alignment_mask * column_crop_mask[None, :]).astype(jnp.float32)
    normalized_rows = apply_layer_norm(alignment_rows, norm_scale_gain, norm_offset_bias).astype(
        jnp.bfloat16
    )
    normalized_columns = apply_layer_norm(
        alignment_columns, norm_scale_gain, norm_offset_bias
    ).astype(jnp.bfloat16)
    left_local_factor = jnp.dot(
        normalized_rows.reshape(-1, ALIGNMENT_WIDTH),
        left_projection_weight,
        preferred_element_type=jnp.float32,
    )
    left_local_factor = (
        left_local_factor.reshape(ALIGNMENT_COUNT, local_rows, PROJECTED_WIDTH)
        * local_mask_weight[:, :, None]
    ).astype(jnp.bfloat16)
    left_outgoing = left_local_factor.transpose(1, 0, 2).reshape(
        local_rows, ALIGNMENT_COUNT * PROJECTED_WIDTH
    )
    right_factor = jnp.dot(
        normalized_columns.reshape(-1, ALIGNMENT_WIDTH),
        right_projection_weight,
        preferred_element_type=jnp.float32,
    )
    right_factor = (
        right_factor.reshape(ALIGNMENT_COUNT, COLUMN_RESIDUES, PROJECTED_WIDTH)
        * column_mask_weight[:, :, None]
    ).astype(jnp.bfloat16)
    denom = jnp.maximum(
        jnp.dot(
            row_mask_weight.T,
            column_mask_weight,
            precision=lax.Precision.HIGHEST,
            preferred_element_type=jnp.float32,
        ),
        1.0,
    )
    weight_back = pair_output_weight.T

    def outer_rows(remaining_rows, rows_denom):
        outer = (
            jnp.einsum(
                "isc,sjd->ijcd", remaining_rows, right_factor, preferred_element_type=jnp.float32
            )
            / rows_denom[:, :, None, None]
        )
        return outer.astype(jnp.bfloat16).reshape(-1, PROJECTED_WIDTH * PROJECTED_WIDTH)

    def outer_grad(rows_grad, rows_denom, row_inputs):
        grad_flat = rows_grad.reshape(-1, PAIR_WIDTH)
        grad_outer = (
            jnp.dot(grad_flat, weight_back, preferred_element_type=jnp.float32)
            / rows_denom.reshape(-1, 1)
        ).astype(jnp.bfloat16)
        return (
            grad_flat,
            grad_outer.reshape(row_inputs, COLUMN_RESIDUES, PROJECTED_WIDTH, PROJECTED_WIDTH),
        )

    def make_step():

        def step(carry, item):
            weight_sum, right_sum = carry
            remaining_rows, rows_denom, rows_grad = item
            flat = outer_rows(remaining_rows, rows_denom)
            grad_flat, grad_four = outer_grad(rows_grad, rows_denom, row_block_inputs)
            weight_sum = weight_sum + jnp.einsum(
                "nc,np->cp", flat, grad_flat, preferred_element_type=jnp.float32
            )
            right_sum = right_sum + jnp.einsum(
                "ijcd,isc->sjd", grad_four, remaining_rows, preferred_element_type=jnp.float32
            )
            extra = ()
            extra = extra + (
                jnp.einsum(
                    "ijcd,sjd->isc", grad_four, right_factor, preferred_element_type=jnp.float32
                ),
            )
            return ((weight_sum, right_sum), extra)

        return step

    mask_count_total = SLAB_ROW_COUNT // row_block_inputs
    denom_blocks = denom.reshape(mask_count_total, row_block_inputs, COLUMN_RESIDUES)
    grad_blocks = pair_update_gradient.reshape(
        mask_count_total, row_block_inputs, COLUMN_RESIDUES, PAIR_WIDTH
    )
    start_index = (
        jnp.zeros((PROJECTED_WIDTH * PROJECTED_WIDTH, PAIR_WIDTH), jnp.float32),
        jnp.zeros((ALIGNMENT_COUNT, COLUMN_RESIDUES, PROJECTED_WIDTH), jnp.float32),
    )
    current_piece = lax.all_gather(left_outgoing, "col", axis=0, tiled=True)
    row_inputs = current_piece.shape[0]
    remaining_rows = current_piece.reshape(row_inputs, ALIGNMENT_COUNT, PROJECTED_WIDTH)
    rows_denom = denom
    pair = (
        jnp.dot(
            outer_rows(remaining_rows, rows_denom),
            pair_output_weight,
            preferred_element_type=jnp.float32,
        )
        + pair_output_bias
    )
    pair_out = pair.astype(jnp.bfloat16).reshape(row_inputs, COLUMN_RESIDUES, PAIR_WIDTH)
    collected_blocks = lax.all_gather(left_outgoing, "col", axis=0, tiled=True)
    left_factor_blocks = collected_blocks.reshape(
        mask_count_total, row_block_inputs, ALIGNMENT_COUNT, PROJECTED_WIDTH
    )
    (weight_sum, right_sum), step_outputs = lax.scan(
        make_step(), start_index, (left_factor_blocks, denom_blocks, grad_blocks)
    )
    left_product_terms = step_outputs[0].reshape(SLAB_ROW_COUNT, ALIGNMENT_COUNT * PROJECTED_WIDTH)
    left_total_sum = lax.psum_scatter(left_product_terms, "col", scatter_dimension=0, tiled=True)
    left_total_sum = left_total_sum.reshape(local_rows, ALIGNMENT_COUNT, PROJECTED_WIDTH).transpose(
        1, 0, 2
    )
    left_side_gradient = (left_total_sum * local_mask_weight[:, :, None]).astype(jnp.bfloat16)
    right_side_gradient = (right_sum * column_mask_weight[:, :, None]).astype(jnp.bfloat16)
    projected_left = jnp.einsum(
        "nm,nc->mc",
        normalized_rows.reshape(-1, ALIGNMENT_WIDTH),
        left_side_gradient.reshape(-1, PROJECTED_WIDTH),
        preferred_element_type=jnp.float32,
    )
    projected_right = jnp.einsum(
        "nm,nc->mc",
        normalized_columns.reshape(-1, ALIGNMENT_WIDTH),
        right_side_gradient.reshape(-1, PROJECTED_WIDTH),
        preferred_element_type=jnp.float32,
    )
    proj_terms = jnp.concatenate([projected_left, projected_right], axis=1)
    grad_pair_weight, grad_proj = (
        lax.psum_scatter(weight_sum, "col", scatter_dimension=0, tiled=True),
        lax.psum_scatter(proj_terms, "col", scatter_dimension=0, tiled=True),
    )
    normalized_row_gradient = jnp.dot(
        left_side_gradient.reshape(-1, PROJECTED_WIDTH),
        left_projection_weight.T,
        preferred_element_type=jnp.float32,
    ).reshape(ALIGNMENT_COUNT, local_rows, ALIGNMENT_WIDTH)
    normalized_column_gradient = jnp.dot(
        right_side_gradient.reshape(-1, PROJECTED_WIDTH),
        right_projection_weight.T,
        preferred_element_type=jnp.float32,
    ).reshape(ALIGNMENT_COUNT, COLUMN_RESIDUES, ALIGNMENT_WIDTH)
    unused_result, row_back_grads = jax.vjp(
        lambda value_array: apply_layer_norm(value_array, norm_scale_gain, norm_offset_bias),
        alignment_rows.astype(jnp.float32),
    )
    unused_result, column_back_grads = jax.vjp(
        lambda value_array: apply_layer_norm(value_array, norm_scale_gain, norm_offset_bias),
        alignment_columns.astype(jnp.float32),
    )
    grad_rows = row_back_grads(normalized_row_gradient)[0].astype(jnp.bfloat16)
    grad_cols = column_back_grads(normalized_column_gradient)[0].astype(jnp.bfloat16)
    return (pair_out, grad_rows, grad_cols, grad_pair_weight, grad_proj)


def solution(mesh):
    placed = (
        P("parts", "col", None),
        P("parts", "col", None),
        P("parts", None),
        P("parts"),
        P("parts", "col"),
        P(("parts", "col")),
        P(),
        P(),
        P(),
        P(),
        P(),
        P(),
        P("parts", "col", None),
    )
    return jax.shard_map(
        per_device,
        mesh=mesh,
        in_specs=placed,
        out_specs=(
            P("parts", "col", None),
            P("parts", "col", None),
            P("parts", "col", None),
            P(("parts", "col"), None),
            P(("parts", "col"), None),
        ),
        check_vma=False,
    )
```

profile of v0, /device:TPU:0, one launch (start us, length us, event | category | flops | bytes accessed | tf_op | source)
XLA Modules:
  0.0 399.0 jit_solution(2750851517956724560)
XLA Ops:
  7.3 0.9 multiply_convert_fusion.4
  8.2 0.1 copy.101
  8.3 0.8 multiply_convert_fusion.3
  9.1 0.1 convolution_maximum_fusion
  9.3 0.5 copy-done.36
  9.9 1.1 convert_reduce_fusion.1
  11.0 1.2 fusion.35
  12.2 1.3 convert_reduce_fusion
  13.5 1.4 fusion.26
  15.0 0.6 copy-done.23
  15.5 1.3 fusion.25
  16.9 0.2 reshape.128
  17.1 0.5 fusion.23
  17.6 0.9 copy.110
  18.5 0.8 copy.108
  19.4 24.6 %all_gather.4 = bf16[128,2048]{1,0:T(8,128)(2,1)S(1)} all-gather(bf16[8,2048]{1,0:T(8,128)(2,1)S(1)} %reshape.128), channel_id=1, replica_groups=mesh['parts'=2,'col'=16] {'col'}, dimensions={0}, use_global_device_ids=true | all-gather | bytes 557056 | tf_op jit(solution)/shard_map/all_gather | solution.py:137
  43.9 0.3 copy.103
  44.2 0.4 reshape.132
  44.7 2.3 copy.109
  47.0 168.8 %while.15 = (s32[]{:T(128)}, f32[1024,128]{1,0:T(8,128)S(1)}, f32[64,16,32]{0,2,1:T(8,128)}, f32[2,64,64,32]{1,0,3,2:T(2,128)}, bf16[2,64,64,32]{2,1,3,0:T(8,128...) while((s32[]{:T(128)}, f32[1024,128]{1,0:T(8,128)S(1)}, ...), condition=%wide.region_5.6_spmd.clone, body=%wide.region_4.5_spmd.clone.sunk | while | flops 944046080 | bytes 43880792 | solution.py:154
  47.2 0.1 copy.161
  47.4 3.1 divide_convert_fusion.3
  50.5 3.3 fusion.90
  53.7 13.4 %copy.160 = bf16[64,16,32,32]{3,2,1,0:T(8,128)(2,1)} copy(bf16[64,16,32,32]{0,3,1,2:T(8,128)(2,1)} %fusion.90) | data formatting | bytes 4194304 | tf_op jit(solution)/shard_map/while/body/eval_jaxpr/convert_element_type | solution.py:92
  67.1 11.3 %reshape.156 = bf16[1024,1024]{1,0:T(8,128)(2,1)S(1)} reshape(bf16[64,16,32,32]{3,2,1,0:T(8,128)(2,1)} %copy.160) | data formatting | bytes 4194304 | tf_op jit(solution)/shard_map/while/body/eval_jaxpr/reshape | solution.py:92
  78.4 0.8 convolution_add_fusion.3
  79.3 11.1 %reshape.157 = bf16[64,16,32,32]{3,2,1,0:T(8,128)(2,1)} reshape(bf16[1024,1024]{1,0:T(8,128)(2,1)} %divide_convert_fusion.3) | data formatting | bytes 4194304 | tf_op jit(solution)/shard_map/while/body/eval_jaxpr/reshape | solution.py:102
  90.4 13.0 %fusion.91 = f32[64,16,32]{0,2,1:T(8,128)S(1)} fusion(bf16[64,16,32,32]{3,2,1,0:T(8,128)(2,1)} %reshape.157, bf16[2,64,64,32]{2,1,3,0:T(8,128)(2,1)S(1)} %copy-done.10, s32[]{:T(128)S(6)} %copy.168, f32[64,16,32]{0,2,1:T(8,128)S(1)} %copy-done.25, pred[]{:T(512)S(6)} %compare.3), kind=kOutput, calls=%fused_computation.8.clone.1 | convolution fusion | flops 134283264 | bytes 3014661 | tf_op jit(solution)/shard_map/while/body/eval_jaxpr/ijcd,isc->sjd/dot_general | solution.py:115
  103.5 1.7 convolution_bitcast_fusion.5
  105.2 0.8 copy.162
  106.0 25.5 %dynamic_update_slice.6 = f32[2,64,64,32]{1,0,3,2:T(2,128)} dynamic-update-slice(f32[2,64,64,32]{1,0,3,2:T(2,128)} %get-tuple-element.248, f32[1,64,64,32]{1,0,3,2:T(1,128)S(1)} %copy.162, s32[]{:T(128)S(6)} %copy.168, s32[]{:T(128)} %constant.21.clone.1..sunk, s32[]{:T(128)} %constant.21.clone.1..sunk, s32[]{:T(128)} %constant.21.clone.1..sunk) | dynamic-update-slice | bytes 1048580 | tf_op jit(solution)/shard_map/while/body/jit(dynamic_update_index_in_dim)/dynamic_update_slice | solution.py:154
  131.5 0.1 copy.161
  131.7 3.1 divide_convert_fusion.3
  134.8 3.3 fusion.90
  138.0 13.4 %copy.160 = bf16[64,16,32,32]{3,2,1,0:T(8,128)(2,1)} copy(bf16[64,16,32,32]{0,3,1,2:T(8,128)(2,1)} %fusion.90) | data formatting | bytes 4194304 | tf_op jit(solution)/shard_map/while/body/eval_jaxpr/convert_element_type | solution.py:92
  151.4 11.3 %reshape.156 = bf16[1024,1024]{1,0:T(8,128)(2,1)S(1)} reshape(bf16[64,16,32,32]{3,2,1,0:T(8,128)(2,1)} %copy.160) | data formatting | bytes 4194304 | tf_op jit(solution)/shard_map/while/body/eval_jaxpr/reshape | solution.py:92
  162.7 0.8 convolution_add_fusion.3
  163.6 11.1 %reshape.157 = bf16[64,16,32,32]{3,2,1,0:T(8,128)(2,1)} reshape(bf16[1024,1024]{1,0:T(8,128)(2,1)} %divide_convert_fusion.3) | data formatting | bytes 4194304 | tf_op jit(solution)/shard_map/while/body/eval_jaxpr/reshape | solution.py:102
  174.7 13.0 %fusion.91 = f32[64,16,32]{0,2,1:T(8,128)S(1)} fusion(bf16[64,16,32,32]{3,2,1,0:T(8,128)(2,1)} %reshape.157, bf16[2,64,64,32]{2,1,3,0:T(8,128)(2,1)S(1)} %copy-done.10, s32[]{:T(128)S(6)} %copy.168, f32[64,16,32]{0,2,1:T(8,128)S(1)} %copy-done.25, pred[]{:T(512)S(6)} %compare.3), kind=kOutput, calls=%fused_computation.8.clone.1 | convolution fusion | flops 134283264 | bytes 3014661 | tf_op jit(solution)/shard_map/while/body/eval_jaxpr/ijcd,isc->sjd/dot_general | solution.py:115
  187.8 1.7 convolution_bitcast_fusion.5
  189.5 0.8 copy.162
  190.3 25.5 %dynamic_update_slice.6 = f32[2,64,64,32]{1,0,3,2:T(2,128)} dynamic-update-slice(f32[2,64,64,32]{1,0,3,2:T(2,128)} %get-tuple-element.248, f32[1,64,64,32]{1,0,3,2:T(1,128)S(1)} %copy.162, s32[]{:T(128)S(6)} %copy.168, s32[]{:T(128)} %constant.21.clone.1..sunk, s32[]{:T(128)} %constant.21.clone.1..sunk, s32[]{:T(128)} %constant.21.clone.1..sunk) | dynamic-update-slice | bytes 1048580 | tf_op jit(solution)/shard_map/while/body/jit(dynamic_update_index_in_dim)/dynamic_update_slice | solution.py:154
  215.8 2.8 reshape.135
  218.7 1.3 copy.128
  220.1 0.7 reduce-scatter.8.cloned.1.call-update
  220.9 0.3 copy.117
  221.3 0.8 convolution_bitcast_fusion.2
  222.1 0.5 fusion.30
  222.7 0.6 fusion.42
  223.4 1.4 add_convert_fusion
  224.8 3.2 fusion.17
  228.0 23.0 %copy.106 = bf16[128,16,32,32]{3,2,1,0:T(8,128)(2,1)} copy(bf16[128,16,32,32]{0,3,2,1:T(8,128)(2,1)} %fusion.17) | data formatting | bytes 8388608 | tf_op jit(solution)/shard_map/convert_element_type | solution.py:92
  251.1 23.3 %reshape.130 = bf16[2048,1024]{1,0:T(8,128)(2,1)} reshape(bf16[128,16,32,32]{3,2,1,0:T(8,128)(2,1)} %copy.106) | data formatting | bytes 8388608 | tf_op jit(solution)/shard_map/reshape | solution.py:92
  274.4 4.3 %fusion.18 = bf16[2048,128]{1,0:T(8,128)(2,1)} fusion(bf16[2048,1024]{1,0:T(8,128)(2,1)} %reshape.130, bf16[1024,128]{1,0:T(8,128)(2,1)S(1)} %copy-done.31, f32[128]{0:T(128)S(1)} %copy-done.43), kind=kOutput, calls=%fused_computation.22 | convolution fusion | flops 537395200 | bytes 4981248 | tf_op jit(solution)/shard_map/dot_general | solution.py:142
  278.7 1.2 copy.129
  279.9 0.6 copy.114
  280.6 0.1 copy.116
  280.7 0.4 convolution_bitcast_fusion.3
  281.1 0.8 copy.130
  281.9 0.3 fusion.39
  282.2 0.4 fusion.46
  282.6 1.0 add_convert_fusion.1
  283.6 50.7 %reduce-scatter.8.cloned.1.call-done = f32[64,128]{1,0:T(8,128)} async-done(((f32[1024,128]{1,0:T(8,128)}), f32[64,128]{1,0:T(8,128)}) %reduce-scatter.8.cloned.1.call-update) | async-done | bytes 32784 | tf_op jit(solution)/shard_map/reduce_scatter | solution.py:178
  334.3 58.2 %reduce-scatter.12.cloned.1.call-done = f32[16,64]{1,0:T(8,128)} async-done(((f32[256,64]{1,0:T(8,128)}), f32[16,64]{1,0:T(8,128)}) %reduce-scatter.12.cloned.1.call-update) | async-done | bytes 4112
  (130 shorter events, 1.0 us)
Async XLA Ops:
  7.2 9.9 %copy-start = (bf16[256,32]{0,1:T(8,128)(2,1)S(1)}, bf16[256,32]{0,1:T(8,128)(2,1)}, u32[]{:S(2)}) copy-start(bf16[256,32]{0,1:T(8,128)(2,1)} %param.24) | copy-start | bytes 49156
  7.2 9.9 %copy-start.3 = (bf16[64,16,256]{2,1,0:T(8,128)(2,1)S(1)}, bf16[64,16,256]{2,1,0:T(8,128)(2,1)}, u32[]{:S(2)}) copy-start(bf16[64,16,256]{2,1,0:T(8,128)(2,1)} %param.16) | copy-start | bytes 1572868
  7.2 9.9 %copy-start.39 = (f32[256]{0:T(256)S(1)}, f32[256]{0:T(256)}, u32[]{:S(2)}) copy-start(f32[256]{0:T(256)} %param.21) | copy-start | bytes 3076
  7.2 9.9 %copy-start.41 = (f32[256]{0:T(256)S(1)}, f32[256]{0:T(256)}, u32[]{:S(2)}) copy-start(f32[256]{0:T(256)} %param.22) | copy-start | bytes 3076
  7.2 11.3 %copy-start.30 = (bf16[1024,128]{1,0:T(8,128)(2,1)S(1)}, bf16[1024,128]{1,0:T(8,128)(2,1)}, u32[]{:S(2)}) copy-start(bf16[1024,128]{1,0:T(8,128)(2,1)} %param.25) | copy-start | bytes 786436
  7.2 271.5 %reduce-scatter.10.cloned.1.call-start = ((), (), s32[]{:S(2)}) async-start(), calls=%async_computation.4 | async-start | bytes 1114112
  8.3 36.0 %copy-start.32 = (f32[64,16]{1,0:T(8,128)}, f32[64,16]{1,0:T(8,128)S(1)}, u32[]{:S(2)}) copy-start(f32[64,16]{1,0:T(8,128)S(1)} %copy.101) | copy-start | bytes 12292
  9.1 0.8 copy-start.15
  9.2 0.6 copy-start.36
  11.0 32.9 %copy-start.13 = (f32[64,8]{1,0:T(8,128)}, f32[64,8]{1,0:T(8,128)S(1)}, u32[]{:S(2)}) copy-start(f32[64,8]{1,0:T(8,128)S(1)} %broadcast_multiply_fusion) | copy-start | bytes 6148
  12.2 31.7 %copy-start.19 = (f32[64,8]{1,0:T(8,128)}, f32[64,8]{1,0:T(8,128)S(1)}, u32[]{:S(2)}) copy-start(f32[64,8]{1,0:T(8,128)S(1)} %fusion.35) | copy-start | bytes 6148
  12.2 31.7 %copy-start.17 = (f32[64,8]{1,0:T(8,128)}, f32[64,8]{1,0:T(8,128)S(1)}, u32[]{:S(2)}) copy-start(f32[64,8]{1,0:T(8,128)S(1)} %fusion.51) | copy-start | bytes 6148
  13.5 31.1 %copy-start.11 = (f32[64,16]{1,0:T(8,128)}, f32[64,16]{1,0:T(8,128)S(1)}, u32[]{:S(2)}) copy-start(f32[64,16]{1,0:T(8,128)S(1)} %broadcast_multiply_fusion.1) | copy-start | bytes 12292
  14.9 0.6 copy-start.23
  15.5 31.4 %copy-start.21 = (f32[64,16]{1,0:T(8,128)}, f32[64,16]{1,0:T(8,128)S(1)}, u32[]{:S(2)}) copy-start(f32[64,16]{1,0:T(8,128)S(1)} %fusion.50) | copy-start | bytes 12292
  16.9 30.1 %copy-start.6 = (bf16[128,16,128]{2,1,0:T(8,128)(2,1)S(1)}, bf16[128,16,128]{2,1,0:T(8,128)(2,1)}, u32[]{:S(2)}) copy-start(bf16[128,16,128]{2,1,0:T(8,128)(2,1)} %param.27) | copy-start | bytes 1572868
  17.6 26.3 %copy-start.28 = (bf16[64,16,32]{2,1,0:T(8,128)(2,1)}, bf16[64,16,32]{2,1,0:T(8,128)(2,1)S(1)}, u32[]{:S(2)}) copy-start(bf16[64,16,32]{2,1,0:T(8,128)(2,1)S(1)} %fusion.23) | copy-start | bytes 196612
  44.2 2.7 copy-start.7
  47.4 3.1 copy-start.9
  47.4 3.1 copy-start.34
  79.3 11.1 %copy-start.10 = (bf16[2,64,64,32]{2,1,3,0:T(8,128)(2,1)S(1)}, bf16[2,64,64,32]{2,1,3,0:T(8,128)(2,1)}, u32[]{:S(2)}) copy-start(bf16[2,64,64,32]{2,1,3,0:T(8,128)(2,1)} %get-tuple-element.260) | copy-start | bytes 1572868 | tf_op jit(solution)/shard_map/while
  79.3 11.1 %copy-start.25 = (f32[64,16,32]{0,2,1:T(8,128)S(1)}, f32[64,16,32]{0,2,1:T(8,128)}, u32[]{:S(2)}) copy-start(f32[64,16,32]{0,2,1:T(8,128)} %get-tuple-element.247) | copy-start | bytes 393220 | tf_op jit(solution)/shard_map/while
  90.4 13.1 %copy-start.1 = (bf16[64,16,32,32]{3,2,1,0:T(8,128)(2,1)S(1)}, bf16[64,16,32,32]{3,2,1,0:T(8,128)(2,1)}, u32[]{:S(2)}) copy-start(bf16[64,16,32,32]{3,2,1,0:T(8,128)(2,1)} %reshape.157) | copy-start | bytes 6291460 | tf_op jit(solution)/shard_map/while
  90.4 13.1 %copy-start.35 = (bf16[64,16,32]{0,2,1:T(8,128)(2,1)S(1)}, bf16[64,16,32]{0,2,1:T(8,128)(2,1)}, u32[]{:S(2)}) copy-start(bf16[64,16,32]{0,2,1:T(8,128)(2,1)} %get-tuple-element.261) | copy-start | bytes 196612 | tf_op jit(solution)/shard_map/while
  103.5 1.7 copy-start.26
  131.7 3.1 copy-start.9
  131.7 3.1 copy-start.34
  163.6 11.1 %copy-start.10 = (bf16[2,64,64,32]{2,1,3,0:T(8,128)(2,1)S(1)}, bf16[2,64,64,32]{2,1,3,0:T(8,128)(2,1)}, u32[]{:S(2)}) copy-start(bf16[2,64,64,32]{2,1,3,0:T(8,128)(2,1)} %get-tuple-element.260) | copy-start | bytes 1572868 | tf_op jit(solution)/shard_map/while
  163.6 11.1 %copy-start.25 = (f32[64,16,32]{0,2,1:T(8,128)S(1)}, f32[64,16,32]{0,2,1:T(8,128)}, u32[]{:S(2)}) copy-start(f32[64,16,32]{0,2,1:T(8,128)} %get-tuple-element.247) | copy-start | bytes 393220 | tf_op jit(solution)/shard_map/while
  174.7 13.1 %copy-start.1 = (bf16[64,16,32,32]{3,2,1,0:T(8,128)(2,1)S(1)}, bf16[64,16,32,32]{3,2,1,0:T(8,128)(2,1)}, u32[]{:S(2)}) copy-start(bf16[64,16,32,32]{3,2,1,0:T(8,128)(2,1)} %reshape.157) | copy-start | bytes 6291460 | tf_op jit(solution)/shard_map/while
  174.7 13.1 %copy-start.35 = (bf16[64,16,32]{0,2,1:T(8,128)(2,1)S(1)}, bf16[64,16,32]{0,2,1:T(8,128)(2,1)}, u32[]{:S(2)}) copy-start(bf16[64,16,32]{0,2,1:T(8,128)(2,1)} %get-tuple-element.261) | copy-start | bytes 196612 | tf_op jit(solution)/shard_map/while
  187.8 1.7 copy-start.26
  215.8 4.3 %copy-start.2 = (f32[1024,128]{1,0:T(8,128)}, f32[1024,128]{1,0:T(8,128)S(1)}, u32[]{:S(2)}) copy-start(f32[1024,128]{1,0:T(8,128)S(1)} %get-tuple-element.56) | copy-start | bytes 1572868
  215.8 5.1 %copy-start.16 = (f32[64,128]{1,0:T(8,128)S(1)}, f32[64,128]{1,0:T(8,128)}, u32[]{:S(2)}) copy-start(f32[64,128]{1,0:T(8,128)} %copy-done.15) | copy-start | bytes 98308
  215.8 5.2 %copy-start.27 = (f32[64,16,32]{0,2,1:T(8,128)S(1)}, f32[64,16,32]{0,2,1:T(8,128)}, u32[]{:S(2)}) copy-start(f32[64,16,32]{0,2,1:T(8,128)} %get-tuple-element.55) | copy-start | bytes 393220
  215.8 5.5 %copy-start.4 = (bf16[64,16,256]{2,1,0:T(8,128)(2,1)S(1)}, bf16[64,16,256]{2,1,0:T(8,128)(2,1)}, u32[]{:S(2)}) copy-start(bf16[64,16,256]{2,1,0:T(8,128)(2,1)} %param.16) | copy-start | bytes 1572868
  215.8 5.4 %copy-start.12 = (f32[64,16]{1,0:T(8,128)S(1)}, f32[64,16]{1,0:T(8,128)}, u32[]{:S(2)}) copy-start(f32[64,16]{1,0:T(8,128)} %copy-done.11) | copy-start | bytes 12292
  215.8 5.4 %copy-start.22 = (f32[64,16]{1,0:T(8,128)S(1)}, f32[64,16]{1,0:T(8,128)}, u32[]{:S(2)}) copy-start(f32[64,16]{1,0:T(8,128)} %copy-done.21) | copy-start | bytes 12292
  215.8 5.4 %copy-start.33 = (f32[64,16]{1,0:T(8,128)S(1)}, f32[64,16]{1,0:T(8,128)}, u32[]{:S(2)}) copy-start(f32[64,16]{1,0:T(8,128)} %copy-done.32) | copy-start | bytes 12292
  215.8 5.4 %copy-start.40 = (f32[256]{0:T(256)S(1)}, f32[256]{0:T(256)}, u32[]{:S(2)}) copy-start(f32[256]{0:T(256)} %param.21) | copy-start | bytes 3076
  215.8 5.4 %copy-start.42 = (f32[256]{0:T(256)S(1)}, f32[256]{0:T(256)}, u32[]{:S(2)}) copy-start(f32[256]{0:T(256)} %param.22) | copy-start | bytes 3076
  218.7 4.0 %copy-start.24 = (f32[64,16]{1,0:T(8,128)S(1)}, f32[64,16]{1,0:T(8,128)}, u32[]{:S(2)}) copy-start(f32[64,16]{1,0:T(8,128)} %copy-done.23) | copy-start | bytes 12292
  220.0 114.3 %reduce-scatter.8.cloned.1.call-start = ((), (), s32[]{:S(2)}) async-start(), calls=%async_computation.3 | async-start | bytes 557056 | tf_op jit(solution)/shard_map/reduce_scatter | solution.py:178
  220.8 171.7 %reduce-scatter.12.cloned.1.call-start = ((), (), s32[]{:S(2)}) async-start(), calls=%async_computation.5 | async-start | bytes 139264
  221.3 3.5 copy-start.8
  221.3 3.5 copy-start.29
  221.3 3.5 copy-start.37
  251.1 23.3 %copy-start.31 = (bf16[1024,128]{1,0:T(8,128)(2,1)S(1)}, bf16[1024,128]{1,0:T(8,128)(2,1)}, u32[]{:S(2)}) copy-start(bf16[1024,128]{1,0:T(8,128)(2,1)} %param.25) | copy-start | bytes 786436
  251.1 23.3 %copy-start.43 = (f32[128]{0:T(128)S(1)}, f32[128]{0:T(128)}, u32[]{:S(2)}) copy-start(f32[128]{0:T(128)} %param.26) | copy-start | bytes 1540
  274.4 6.3 %copy-start.5 = (bf16[64,8,256]{2,1,0:T(8,128)(2,1)S(1)}, bf16[64,8,256]{2,1,0:T(8,128)(2,1)}, u32[]{:S(2)}) copy-start(bf16[64,8,256]{2,1,0:T(8,128)(2,1)} %param.15) | copy-start | bytes 786436
  274.4 6.3 %copy-start.14 = (f32[64,8]{1,0:T(8,128)S(1)}, f32[64,8]{1,0:T(8,128)}, u32[]{:S(2)}) copy-start(f32[64,8]{1,0:T(8,128)} %copy-done.13) | copy-start | bytes 6148
  274.4 6.3 %copy-start.18 = (f32[64,8]{1,0:T(8,128)S(1)}, f32[64,8]{1,0:T(8,128)}, u32[]{:S(2)}) copy-start(f32[64,8]{1,0:T(8,128)} %copy-done.17) | copy-start | bytes 6148
  274.4 7.4 %copy-start.38 = (bf16[256,32]{0,1:T(8,128)(2,1)S(1)}, bf16[256,32]{0,1:T(8,128)(2,1)}, u32[]{:S(2)}) copy-start(bf16[256,32]{0,1:T(8,128)(2,1)} %param.23) | copy-start | bytes 49156
  274.4 7.7 %copy-start.20 = (f32[64,8]{1,0:T(8,128)S(1)}, f32[64,8]{1,0:T(8,128)}, u32[]{:S(2)}) copy-start(f32[64,8]{1,0:T(8,128)} %copy-done.19) | copy-start | bytes 6148
Sparse Core Ops, SparseCore 0:
  220.2 54.6 reduce-scatter.9
  279.4 54.8 reduce-scatter.7
  338.4 54.0 reduce-scatter.11
where the time goes:
time: 405 us; the launch traced here: 399 us
  local copies, waits for them, and re-layouts  185 us (46%)
  waiting for transfers between devices  110 us (27%)
  matrix products  55.1 us (14%)
  blocking collectives  24.6 us (6%)
  between operations  14.4 us (4%)
  other arithmetic  10.2 us (3%)
    unnamed x5, waiting for transfers between devices  58.9 us
    dynamic_update_slice x4, local copies, waits for them, and re-layouts, per_device(): lax.scan(make_step(), start_index, (left_factor_blocks, denom_blocks, gra...  52.6 us
    reduce_scatter x1, waiting for transfers between devices, per_device(): lax.psum_scatter(weight_sum, 'col', scatter_dimension=0, tiled=True)  50.7 us
    convert_element_type x3, local copies, waits for them, and re-layouts, outer_rows(): outer.astype(jnp.bfloat16).reshape(-1, PROJECTED_WIDTH * PROJECTED_WIDTH)  49.8 us
    reshape x3, local copies, waits for them, and re-layouts, outer_rows(): outer.astype(jnp.bfloat16).reshape(-1, PROJECTED_WIDTH * PROJECTED_WIDTH)  46 us
    dot_general x2, matrix products, step(): jnp.einsum('ijcd,isc->sjd', grad_four, remaining_rows, preferred_element_...  26.1 us
    all_gather x1, blocking collectives, per_device(): current_piece = lax.all_gather(left_outgoing, 'col', axis=0, tiled=True)  24.6 us
    reshape x2, local copies, waits for them, and re-layouts, outer_grad(): grad_outer.reshape(row_inputs, COLUMN_RESIDUES, PROJECTED_WIDTH, PROJECTE...  22.2 us
  transfers between devices with their start and end apart: 3, of which 2 were waited for; matrix products, arithmetic and copies ran while one was open for 16% of the time, Pallas kernels for 0%

commit v1 on v0

v1 whole, which is shorter than its diff:
```python
import functools

import jax
import jax.numpy as jnp
from jax import lax
from jax.experimental import pallas as pl
from jax.experimental.pallas import tpu as pltpu
from jax.sharding import PartitionSpec as P

F32 = jnp.float32
BF16 = jnp.bfloat16
M = 256
C = 32
PW = 128
S = 64
NI = 128
J = 16
EPS = 1e-05
VMEM_LIMIT = 48 * 1024 * 1024

NN = (((1,), (0,)), ((), ()))
NT = (((1,), (1,)), ((), ()))
TN = (((0,), (0,)), ((), ()))


def dot(a, b, dims=NN):
    return lax.dot_general(a, b, dims, preferred_element_type=F32)


def eye(n):
    r = lax.broadcasted_iota(jnp.int32, (n, n), 0)
    c = lax.broadcasted_iota(jnp.int32, (n, n), 1)
    return (r == c).astype(F32).astype(BF16)


def turned(a):
    return dot(eye(a.shape[1]), a, NT)


def row_weights(sm_ref, sc_ref):
    return (sm_ref[...] * sc_ref[...]).astype(F32).astype(BF16)


def col_weights_t(cm_ref, cc_ref):
    return turned((cm_ref[...] * cc_ref[...]).astype(F32).astype(BF16))


def local_weights_t(rw, lr):
    pad = max(lr, 8)
    first = lax.axis_index("col") * lr
    r = lax.broadcasted_iota(jnp.int32, (pad, NI), 0) + first
    c = lax.broadcasted_iota(jnp.int32, (pad, NI), 1)
    return dot((r == c).astype(F32).astype(BF16), rw, NT)


def normalize(x):
    mean = jnp.mean(x, axis=-1, keepdims=True)
    center = x - mean
    rstd = lax.rsqrt(jnp.mean(center * center, axis=-1, keepdims=True) + EPS)
    return center * rstd, rstd


def put_halves(ref, rows, value):
    ref[0, 0:rows, :] = value[:, 0:128]
    ref[1, 0:rows, :] = value[:, 128:256]


def get_halves(ref, start, stride):
    return jnp.concatenate(
        [ref[h, pl.ds(start, S, stride), :] for h in range(2)], axis=1
    )


def project_kernel(lr, xr, xc, sm, sc, cm, cc, gain, bias, wl, wr, left, right, buf):
    rw = row_weights(sm, sc)
    lw = local_weights_t(rw, lr)
    cw = col_weights_t(cm, cc)
    for x_ref, w_ref, weights, count, out in ((xc, wr, cw, J, right), (xr, wl, lw, lr, left)):
        w_t = turned(w_ref[...]).astype(BF16)
        xhat, _ = normalize(x_ref[...].astype(F32))
        normed = (xhat * gain[...] + bias[...]).astype(BF16)
        put_halves(buf, S * count, normed.astype(F32))
        for i in range(count):
            part = get_halves(buf, i, count).astype(BF16)
            prod = dot(w_t, part, NT) * weights[i : i + 1, :]
            out[i * C : (i + 1) * C, :] = prod.astype(BF16)


def pair_kernel(
    lic, right, g, w, pbias, sm, sc, cm, cc,
    pair, gw, gl, gr,
    l32, lt, g32, gall, o, gy, p32, gl32,
):
    rw = row_weights(sm, sc)
    cw = col_weights_t(cm, cc)
    denom = jnp.maximum(dot(cw.astype(BF16), rw), 1.0)
    inv = 1.0 / denom
    l32[:, 0:S] = lic[...].astype(F32)
    g32[...] = g[...].astype(F32)
    rt = right[...]
    for c in range(C):
        lt[c * NI : (c + 1) * NI, :] = l32[pl.ds(c, NI, C), :][:, 0:S].astype(BF16)
    wv = w[...]
    for j in range(J):
        gj = g32[pl.ds(j, NI, J), :].astype(BF16)
        gall[j * NI : (j + 1) * NI, :] = gj
        go = (dot(wv, gj, NT) * inv[j : j + 1, :]).astype(BF16)
        for c in range(C):
            gy[j * C : (j + 1) * C, c * NI : (c + 1) * NI] = go[c * C : (c + 1) * C, :]
    for c in range(C):
        y = dot(rt, lt[c * NI : (c + 1) * NI, :], NT)
        for j in range(J):
            o[c * C : (c + 1) * C, j * NI : (j + 1) * NI] = (
                y[j * C : (j + 1) * C, :] * inv[j : j + 1, :]
            ).astype(BF16)
    r = turned(rt).astype(BF16)
    for c in range(C):
        part = dot(r, gy[:, c * NI : (c + 1) * NI])
        gl32[pl.ds(c, NI, C), :] = jnp.concatenate([part, part], axis=0).T
    gl[...] = gl32[:, 0:S].astype(gl.dtype)
    acc = dot(gy[...], lt[...])
    for j in range(J):
        gr[j * C : (j + 1) * C, :] = (acc[j * C : (j + 1) * C, :] * cw[j : j + 1, :]).astype(BF16)
    gw[...] = dot(o[...], gall[...])
    for j in range(J):
        pj = dot(o[:, j * NI : (j + 1) * NI], wv, TN) + pbias[...]
        p32[pl.ds(j, NI, J), :] = pj
    pair[...] = p32[...].astype(BF16)


def finish_kernel(
    n, lr, glr, gwr, gr, xr, xc, sm, sc, gain, bias, wl, wr,
    grows, gcols, gw, proj, buf, dbuf,
):
    lw = local_weights_t(row_weights(sm, sc), lr)
    gw[...] = jnp.sum(gwr[...].astype(F32), axis=0)
    total = jnp.sum(glr[...].astype(F32), axis=0)
    projs = []
    for x_ref, w_ref, count, out in ((xr, wl, lr, grows), (xc, wr, J, gcols)):
        rows = S * count
        w_t = turned(w_ref[...]).astype(BF16)
        xhat, rstd = normalize(x_ref[...].astype(F32))
        normed = (xhat * gain[...] + bias[...]).astype(BF16)
        put_halves(buf, rows, normed.astype(F32))
        acc = jnp.zeros((C, M), F32)
        for i in range(count):
            if count == J and x_ref is xc:
                gi = gr[i * C : (i + 1) * C, :]
            else:
                gi = (total[i * C : (i + 1) * C, :] * lw[i : i + 1, :]).astype(BF16)
            part = get_halves(buf, i, count).astype(BF16)
            acc = acc + dot(gi, part)
            dn = dot(turned(gi).astype(BF16), w_t)
            dbuf[0, pl.ds(i, S, count), :] = dn[:, 0:128]
            dbuf[1, pl.ds(i, S, count), :] = dn[:, 128:256]
        projs.append(acc)
        dx = jnp.concatenate([dbuf[0, 0:rows, :], dbuf[1, 0:rows, :]], axis=1) * gain[...]
        m1 = jnp.mean(dx, axis=-1, keepdims=True)
        m2 = jnp.mean(dx * xhat, axis=-1, keepdims=True)
        out[...] = ((dx - m1 - xhat * m2) * rstd).astype(BF16)
    both = jnp.concatenate(projs + projs, axis=0)
    proj[...] = both.T[:, 0 : 2 * C]


def greet(n, me):
    barrier = pltpu.get_barrier_semaphore()
    for k in range(1, n):
        pl.semaphore_signal(
            barrier, inc=1, device_id={"col": lax.rem(me + k, n)},
            device_id_type=pl.DeviceIdType.MESH,
        )
    pl.semaphore_wait(barrier, n - 1)


def exchange_kernel(n, whole, count, *refs):
    ins, outs = refs[:count], refs[count : 2 * count]
    send, recv, own = refs[2 * count :]
    me = lax.axis_index("col")
    greet(n, me)
    copies = []
    for k in range(1, n):
        peer = lax.rem(me + k, n)
        for a in range(count):
            copy = pltpu.make_async_remote_copy(
                src_ref=ins[a] if whole else ins[a].at[peer],
                dst_ref=outs[a].at[me],
                send_sem=send.at[a, k],
                recv_sem=recv.at[a, k],
                device_id={"col": peer},
                device_id_type=pl.DeviceIdType.MESH,
            )
            copy.start()
            copies.append(copy)
    for a in range(count):
        copy = pltpu.make_async_copy(ins[a] if whole else ins[a].at[me], outs[a].at[me], own.at[a])
        copy.start()
        copies.append(copy)
    for copy in copies:
        copy.wait()


def exchange(n, whole, cid, *arrays):
    count = len(arrays)
    return pl.pallas_call(
        functools.partial(exchange_kernel, n, whole, count),
        out_shape=[
            jax.ShapeDtypeStruct(((n,) + a.shape) if whole else a.shape, a.dtype) for a in arrays
        ],
        in_specs=[pl.BlockSpec(memory_space=pltpu.VMEM)] * count,
        out_specs=[pl.BlockSpec(memory_space=pltpu.VMEM)] * count,
        scratch_shapes=[
            pltpu.SemaphoreType.DMA((count, n)),
            pltpu.SemaphoreType.DMA((count, n)),
            pltpu.SemaphoreType.DMA((count,)),
        ],
        compiler_params=pltpu.CompilerParams(
            collective_id=cid, has_side_effects=True, vmem_limit_bytes=VMEM_LIMIT
        ),
        name="exchange%d" % cid,
    )(*arrays)


def call(kernel, outs, scratch, *args):
    return pl.pallas_call(
        kernel,
        out_shape=[jax.ShapeDtypeStruct(s, d) for s, d in outs],
        scratch_shapes=[pltpu.VMEM(s, d) for s, d in scratch],
        compiler_params=pltpu.CompilerParams(vmem_limit_bytes=VMEM_LIMIT),
    )(*args)


def per_device(n, xr, xc, sm, sc, cm, cc, gain, bias, wl, wr, w, pbias, g):
    lr = xr.shape[1]
    xr = xr.reshape(S * lr, M)
    xc = xc.reshape(S * J, M)
    sc, cc = sc[None, :], cc[None, :]
    gain, bias, pbias = gain[None, :], bias[None, :], pbias[None, :]
    g = g.reshape(NI * J, PW)
    left, right = call(
        functools.partial(project_kernel, lr),
        [((lr * C, S), BF16), ((J * C, S), BF16)],
        [((2, S * max(J, lr), 128), F32)],
        xr, xc, sm, sc, cm, cc, gain, bias, wl, wr,
    )
    (lic,) = exchange(n, True, 0, left)
    pair, gw, gl, gr = call(
        pair_kernel,
        [((NI * J, PW), BF16), ((C * C, PW), F32), ((NI * C, S), F32), ((J * C, S), BF16)],
        [
            ((NI * C, 128), F32), ((NI * C, S), BF16), ((NI * J, PW), F32), ((NI * J, PW), BF16),
            ((C * C, NI * J), BF16), ((J * C, NI * C), BF16), ((NI * J, PW), F32),
            ((NI * C, 128), F32),
        ],
        lic.reshape(NI * C, S), right, g, w, pbias, sm, sc, cm, cc,
    )
    glr, gwr = exchange(
        n, False, 1, gl.reshape(n, lr * C, S), gw.reshape(n, C * C // n, PW)
    )
    grows, gcols, gw, proj = call(
        functools.partial(finish_kernel, n, lr),
        [((S * lr, M), BF16), ((S * J, M), BF16), ((C * C // n, PW), F32), ((M, 2 * C), F32)],
        [((2, S * max(J, lr), 128), F32)] * 2,
        glr, gwr, gr, xr, xc, sm, sc, gain, bias, wl, wr,
    )
    (prs,) = exchange(n, False, 2, proj.reshape(n, M // n, 2 * C))
    return (
        pair.reshape(NI, J, PW),
        grows.reshape(S, lr, M),
        gcols.reshape(S, J, M),
        gw,
        jnp.sum(prs, axis=0),
    )


def solution(mesh):
    placed = (
        P("parts", "col", None), P("parts", "col", None), P("parts", None), P("parts"),
        P("parts", "col"), P(("parts", "col")), P(), P(), P(), P(), P(), P(),
        P("parts", "col", None),
    )
    return jax.shard_map(
        functools.partial(per_device, mesh.shape["col"]),
        mesh=mesh,
        in_specs=placed,
        out_specs=(
            P("parts", "col", None), P("parts", "col", None), P("parts", "col", None),
            P(("parts", "col"), None), P(("parts", "col"), None),
        ),
        check_vma=False,
    )
```

time: 405 us -> 122 us (0.30); the launches traced: 399 us -> 122 us
  local copies, waits for them, and re-layouts: 185 us -> 7.94 us
  Pallas kernels: 0 us -> 113 us
  waiting for transfers between devices: 110 us -> 0 us
  matrix products: 55.1 us -> 0 us
  blocking collectives: 24.6 us -> 0 us
  between operations: 14.4 us -> 0.82 us
  other arithmetic: 10.2 us -> 0.62 us
    pallas_call x0 -> x6, Pallas kernels: none -> 113 us  [the longest x3 97.5 us: exchange(): pl.pallas_call(functools.partial(exchange_kernel, n, whole, count), out_s...]
    reshape x10 -> x0, local copies, waits for them, and re-layouts: 72.2 us -> none  [the longest x3 46 us: outer_rows(): outer.astype(jnp.bfloat16).reshape(-1, PROJECTED_WIDTH * PROJECTED_WIDTH)]
    unnamed x5 -> x0, waiting for transfers between devices: 58.9 us -> none
    dot_general x19 -> x0, matrix products: 55.1 us -> none  [the longest x2 26.1 us: step(): jnp.einsum('ijcd,isc->sjd', grad_four, remaining_rows, preferred_element_...]
    dynamic_update_slice x4 -> x0, local copies, waits for them, and re-layouts: 52.6 us -> none  [per_device(): lax.scan(make_step(), start_index, (left_factor_blocks, denom_blocks, gra...]
    reduce_scatter x1 -> x0, waiting for transfers between devices: 50.7 us -> none  [per_device(): lax.psum_scatter(weight_sum, 'col', scatter_dimension=0, tiled=True)]
    convert_element_type x6 -> x0, local copies, waits for them, and re-layouts: 50.1 us -> none  [the longest x3 49.8 us: outer_rows(): outer.astype(jnp.bfloat16).reshape(-1, PROJECTED_WIDTH * PROJECTED_WIDTH)]
    all_gather x1 -> x0, blocking collectives: 24.6 us -> none  [per_device(): current_piece = lax.all_gather(left_outgoing, 'col', axis=0, tiled=True)]
  transfers between devices with their start and end apart: 3 -> 0, of which waited for: 2 -> 0; matrix products, arithmetic and copies ran while one was open for 16% -> 0% of each run, Pallas kernels for 0% -> 0%
where the time goes in v1:
time: 122 us
  Pallas kernels  113 us (93%)
  local copies, waits for them, and re-layouts  7.94 us (7%)
    pallas_call x3, Pallas kernels, exchange(): pl.pallas_call(functools.partial(exchange_kernel, n, whole, count), out_s...  97.5 us
    pallas_call x3, Pallas kernels, call(): pl.pallas_call(kernel, out_shape=[jax.ShapeDtypeStruct(s, d) for s, d in...  15 us
    unnamed x37, local copies, waits for them, and re-layouts  7.94 us

profile of v1, /device:TPU:0, one launch (start us, length us, event | category | flops | bytes accessed | tf_op | source)
XLA Modules:
  0.0 121.9 jit_solution(5656544393026964829)
XLA Ops:
  0.6 0.0 copy-start.6
  0.6 0.0 copy-start.16
  0.7 0.0 copy-start.15
  0.7 0.0 copy-start.9
  0.7 0.8 copy.18.cm
  1.5 0.8 copy.19.wl
  2.3 0.8 copy.20.wr
  3.2 0.0 copy-start
  3.2 1.0 copy-done
  4.2 0.0 copy-start.2
  4.2 0.9 copy-done.2
  5.1 0.0 copy-start.5
  5.2 0.8 copy-done.5
  5.9 0.0 copy-start.8
  5.9 0.7 copy-done.8
  6.6 0.0 copy-start.10
  6.6 0.7 copy-done.10
  7.2 0.0 copy-start.12
  7.2 0.7 copy-done.12
  7.9 0.0 copy-start.14
  7.9 0.7 copy-done.14
  8.6 0.0 copy-start.4
  8.6 0.0 copy-start.7
  8.6 1.3 %shard_map.164 = (bf16[256,64]{1,0:T(8,128)(2,1)S(1)}, bf16[512,64]{1,0:T(8,128)(2,1)S(1)}) custom-call(bf16[512,256]{1,0:T(8,128)(2,1)S(1)} %bitcast.19, bf16[1024,256]{1,0:T(8,128)(2,1)S(1)} %bitcast.17, s32[64,128]{1,0:T(8,128)S(1)} %copy-done.5, s32[1,128]{1,0:T(1,128)S(1)} %bitcast.24, s32[64,16]{1,0:T(8,128)S(1)} %copy.18.cm, s32[1,16]{1,0:T(1,128)S(1)} %bitcast.31, ...), custom_call_target="tpu_custom_call" | custom-call | tf_op jit(solution)/shard_map/pallas_call | solution.py:224
  9.8 23.8 %exchange0.1 = bf16[16,256,64]{2,1,0:T(8,128)(2,1)S(1)} custom-call(bf16[256,64]{1,0:T(8,128)(2,1)S(1)} %get-tuple-element.17.refs_0_), custom_call_target="tpu_custom_call" | custom-call | tf_op jit(solution)/shard_map/exchange0/pallas_call | solution.py:204
  33.6 0.0 copy-done.6
  33.6 0.0 copy-done.16
  33.6 0.0 copy-done.15
  33.6 0.0 copy-done.9
  33.7 0.0 copy-done.4
  33.7 0.0 copy-done.7
  33.7 0.0 copy-start.1
  33.7 0.0 copy-start.3
  33.7 0.0 copy-start.11
  33.7 0.0 copy-start.13
  33.7 10.4 %shard_map.165 = (bf16[2048,128]{1,0:T(8,128)(2,1)}, f32[1024,128]{1,0:T(8,128)S(1)}, f32[4096,64]{1,0:T(8,128)S(1)}, bf16[512,64]{1,0:T(8,128)(2,1)S(1)}) custom-call(bf16[4096,64]{1,0:T(8,128)(2,1)S(1)} %bitcast.15, bf16[512,64]{1,0:T(8,128)(2,1)S(1)} %get-tuple-element.18.right, bf16[2048,128]{1,0:T(8,128)(2,1)S(1)} %bitcast.22, ...), custom_call_target="tpu_custom_call" | custom-call | tf_op jit(solution)/shard_map/pallas_call | solution.py:224
  44.1 52.6 %exchange1.1 = (f32[16,256,64]{2,1,0:T(8,128)S(1)}, f32[16,64,128]{2,1,0:T(8,128)S(1)}) custom-call(f32[16,256,64]{2,1,0:T(8,128)S(1)} %bitcast.16, f32[16,64,128]{2,1,0:T(8,128)S(1)} %bitcast.21), custom_call_target="tpu_custom_call" | custom-call | tf_op jit(solution)/shard_map/exchange1/pallas_call | solution.py:204
  96.8 0.0 copy-done.1
  96.8 0.0 copy-done.3
  96.8 0.0 copy-done.11
  96.8 0.0 copy-done.13
  96.8 3.4 %shard_map.166 = (bf16[512,256]{1,0:T(8,128)(2,1)}, bf16[1024,256]{1,0:T(8,128)(2,1)}, f32[64,128]{1,0:T(8,128)}, f32[256,64]{1,0:T(8,128)S(1)}) custom-call(f32[16,256,64]{2,1,0:T(8,128)S(1)} %get-tuple-element.22.glr, f32[16,64,128]{2,1,0:T(8,128)S(1)} %get-tuple-element.23.gwr, bf16[512,64]{1,0:T(8,128)(2,1)S(1)} %get-tuple-element.24.gr, ...), custom_call_target="tpu_custom_call" | custom-call | tf_op jit(solution)/shard_map/pallas_call | solution.py:224
  100.2 21.1 %exchange2.1 = f32[16,16,64]{2,1,0:T(8,128)S(1)} custom-call(f32[16,16,64]{2,1,0:T(8,128)S(1)} %bitcast.23), custom_call_target="tpu_custom_call" | custom-call | tf_op jit(solution)/shard_map/exchange2/pallas_call | solution.py:204
  121.3 0.6 reduce_sum.9
Async XLA Ops:
  0.6 33.0 %copy-start.6 = (s32[64,128]{1,0:T(8,128)S(1)}, s32[64,128]{1,0:T(8,128)}, u32[]{:S(2)}) copy-start(s32[64,128]{1,0:T(8,128)} %sm.5) | copy-start | bytes 98308
  0.6 33.0 %copy-start.16 = (f32[128]{0:T(128)S(1)}, f32[128]{0:T(128)}, u32[]{:S(2)}) copy-start(f32[128]{0:T(128)} %param.24) | copy-start | bytes 1540
  0.7 33.0 %copy-start.15 = (s32[16]{0:T(128)S(1)}, s32[16]{0:T(128)}, u32[]{:S(2)}) copy-start(s32[16]{0:T(128)} %param.18) | copy-start | bytes 196
  0.7 33.0 %copy-start.9 = (s32[128]{0:T(128)S(1)}, s32[128]{0:T(128)}, u32[]{:S(2)}) copy-start(s32[128]{0:T(128)} %param.16) | copy-start | bytes 1540
  3.2 1.0 copy-start
  4.2 0.9 copy-start.2
  5.1 0.8 copy-start.5
  5.9 0.7 copy-start.8
  6.6 0.7 copy-start.10
  7.2 0.7 copy-start.12
  7.9 0.7 copy-start.14
  8.6 25.1 %copy-start.4 = (bf16[128,16,128]{2,1,0:T(8,128)(2,1)S(1)}, bf16[128,16,128]{2,1,0:T(8,128)(2,1)}, u32[]{:S(2)}) copy-start(bf16[128,16,128]{2,1,0:T(8,128)(2,1)} %param.25) | copy-start | bytes 1572868
  8.6 25.1 %copy-start.7 = (bf16[1024,128]{1,0:T(8,128)(2,1)S(1)}, bf16[1024,128]{1,0:T(8,128)(2,1)}, u32[]{:S(2)}) copy-start(bf16[1024,128]{1,0:T(8,128)(2,1)} %w.1) | copy-start | bytes 786436
  33.7 63.1 %copy-start.1 = (bf16[64,16,256]{2,1,0:T(8,128)(2,1)S(1)}, bf16[64,16,256]{2,1,0:T(8,128)(2,1)}, u32[]{:S(2)}) copy-start(bf16[64,16,256]{2,1,0:T(8,128)(2,1)} %param.14) | copy-start | bytes 1572868
  33.7 63.1 %copy-start.3 = (bf16[64,8,256]{2,1,0:T(8,128)(2,1)S(1)}, bf16[64,8,256]{2,1,0:T(8,128)(2,1)}, u32[]{:S(2)}) copy-start(bf16[64,8,256]{2,1,0:T(8,128)(2,1)} %param.13) | copy-start | bytes 786436
  33.7 63.1 %copy-start.11 = (f32[256]{0:T(256)S(1)}, f32[256]{0:T(256)}, u32[]{:S(2)}) copy-start(f32[256]{0:T(256)} %param.19) | copy-start | bytes 3076
  33.7 63.1 %copy-start.13 = (f32[256]{0:T(256)S(1)}, f32[256]{0:T(256)}, u32[]{:S(2)}) copy-start(f32[256]{0:T(256)} %param.20) | copy-start | bytes 3076

commit v2 on v1

v2 whole, which is shorter than its diff:
```python
import functools

import jax
import jax.numpy as jnp
from jax import lax
from jax.experimental import pallas as pl
from jax.experimental.pallas import tpu as pltpu
from jax.sharding import PartitionSpec as P

F32 = jnp.float32
BF16 = jnp.bfloat16
M = 256
C = 32
H = C // 2
PW = 128
S = 64
NI = 128
J = 16
EPS = 1e-05
VMEM_LIMIT = 48 * 1024 * 1024

NN = (((1,), (0,)), ((), ()))
NT = (((1,), (1,)), ((), ()))
TN = (((0,), (0,)), ((), ()))


def dot(a, b, dims=NN):
    return lax.dot_general(a, b, dims, preferred_element_type=F32)


def eye(n):
    r = lax.broadcasted_iota(jnp.int32, (n, n), 0)
    c = lax.broadcasted_iota(jnp.int32, (n, n), 1)
    return (r == c).astype(F32).astype(BF16)


def turned(a):
    return dot(eye(a.shape[1]), a, NT)


def row_weights(sm_ref, sc_ref):
    return (sm_ref[...] * sc_ref[...]).astype(F32).astype(BF16)


def col_weights_t(cmt_ref, cc_ref):
    crop = jnp.broadcast_to(cc_ref[...].astype(F32), (8, J)).astype(BF16)
    return cmt_ref[...].astype(F32) * turned(crop)[:, 0:1]


def local_weights_t(rw, lr):
    pad = max(lr, 8)
    first = lax.axis_index("col") * lr
    r = lax.broadcasted_iota(jnp.int32, (pad, NI), 0) + first
    c = lax.broadcasted_iota(jnp.int32, (pad, NI), 1)
    return dot((r == c).astype(F32).astype(BF16), rw, NT)


def normalize(x):
    mean = jnp.mean(x, axis=-1, keepdims=True)
    center = x - mean
    rstd = lax.rsqrt(jnp.mean(center * center, axis=-1, keepdims=True) + EPS)
    return center * rstd, rstd


def put_halves(ref, rows, value):
    ref[0, 0:rows, :] = value[:, 0:128]
    ref[1, 0:rows, :] = value[:, 128:256]


def get_halves(ref, start, stride):
    return jnp.concatenate(
        [ref[h, pl.ds(start, S, stride), :] for h in range(2)], axis=1
    )


def inverse_denom(cw, rw):
    return 1.0 / jnp.maximum(dot(cw.astype(BF16), rw), 1.0)


def first_kernel(
    lr, xr, xc, sm, sc, cmt, cc, gain, bias, wlt, wrt, g, w,
    left, right, gall, gy, gl, buf, g32, gl32,
):
    rw = row_weights(sm, sc)
    lw = local_weights_t(rw, lr)
    cw = col_weights_t(cmt, cc)
    inv = inverse_denom(cw, rw)
    for x_ref, w_ref, count in ((xc, wrt, J), (xr, wlt, lr)):
        w_t = w_ref[...]
        xhat, _ = normalize(x_ref[...].astype(F32))
        normed = (xhat * gain[...] + bias[...]).astype(BF16)
        put_halves(buf, S * count, normed.astype(F32))
        for i in range(count):
            part = get_halves(buf, i, count).astype(BF16)
            prod = dot(w_t, part, NT)
            if x_ref is xc:
                right[i * C : (i + 1) * C, :] = (prod * cw[i : i + 1, :]).astype(BF16)
            else:
                prod = prod * lw[i : i + 1, :]
                left[i * H : (i + 1) * H, :] = jnp.concatenate(
                    [prod[0:H, :], prod[H:C, :]], axis=1
                ).astype(BF16)
    g32[...] = g[...].astype(F32)
    wv = w[...]
    for j in range(J):
        gj = g32[pl.ds(j, NI, J), :].astype(BF16)
        gall[j * NI : (j + 1) * NI, :] = gj
        go = (dot(wv, gj, NT) * inv[j : j + 1, :]).astype(BF16)
        for c in range(C):
            gy[j * C : (j + 1) * C, c * NI : (c + 1) * NI] = go[c * C : (c + 1) * C, :]
    r = turned(right[...]).astype(BF16)
    for c in range(H):
        low = dot(r, gy[:, c * NI : (c + 1) * NI])
        high = dot(r, gy[:, (c + H) * NI : (c + H + 1) * NI])
        gl32[pl.ds(c, NI, H), :] = jnp.concatenate([low, high], axis=0).T
    gl[...] = gl32[...].astype(BF16)


def middle_kernel(
    n, lr, lic, glr, right, gall, gy, w, pbias, xr, xc, sm, sc, cmt, cc, gain, bias, wlt, wrt,
    pair, gw, grows, gcols, proj, l32, lt, o, p32, buf, dbuf,
):
    rw = row_weights(sm, sc)
    lw = local_weights_t(rw, lr)
    cw = col_weights_t(cmt, cc)
    inv = inverse_denom(cw, rw)
    l32[...] = lic[...].astype(F32)
    rt = right[...]
    zero = jnp.zeros_like(rt)
    rts = (jnp.concatenate([rt, zero], axis=1), jnp.concatenate([zero, rt], axis=1))
    wv = w[...]
    for c in range(H):
        lc = l32[pl.ds(c, NI, H), :].astype(BF16)
        lt[c * NI : (c + 1) * NI, :] = lc
        for h in range(2):
            y = dot(rts[h], lc, NT)
            at = (h * H + c) * C
            for j in range(J):
                o[at : at + C, j * NI : (j + 1) * NI] = (
                    y[j * C : (j + 1) * C, :] * inv[j : j + 1, :]
                ).astype(BF16)
    gw[...] = dot(o[...], gall[...]).astype(BF16)
    for j in range(J):
        pj = dot(o[:, j * NI : (j + 1) * NI], wv, TN) + pbias[...]
        p32[pl.ds(j, NI, J), :] = pj
    pair[...] = p32[...].astype(BF16)
    ltv = lt[...]
    acc_low = dot(gy[:, 0 : H * NI], ltv)
    acc_high = dot(gy[:, H * NI : C * NI], ltv)
    acc = acc_low[:, 0:S] + acc_high[:, S : 2 * S]
    total = jnp.sum(glr[...].astype(F32), axis=0)
    projs = []
    for x_ref, w_ref, count, out in ((xr, wlt, lr, grows), (xc, wrt, J, gcols)):
        rows = S * count
        w_t = w_ref[...]
        xhat, rstd = normalize(x_ref[...].astype(F32))
        normed = (xhat * gain[...] + bias[...]).astype(BF16)
        put_halves(buf, rows, normed.astype(F32))
        ptot = jnp.zeros((C, M), F32)
        for i in range(count):
            if x_ref is xc:
                gi = (acc[i * C : (i + 1) * C, :] * cw[i : i + 1, :]).astype(BF16)
            else:
                ti = total[i * H : (i + 1) * H, :]
                ti = jnp.concatenate([ti[:, 0:S], ti[:, S : 2 * S]], axis=0)
                gi = (ti * lw[i : i + 1, :]).astype(BF16)
            part = get_halves(buf, i, count).astype(BF16)
            ptot = ptot + dot(gi, part)
            dn = dot(turned(gi).astype(BF16), w_t)
            dbuf[0, pl.ds(i, S, count), :] = dn[:, 0:128]
            dbuf[1, pl.ds(i, S, count), :] = dn[:, 128:256]
        projs.append(ptot)
        dx = jnp.concatenate([dbuf[0, 0:rows, :], dbuf[1, 0:rows, :]], axis=1) * gain[...]
        m1 = jnp.mean(dx, axis=-1, keepdims=True)
        m2 = jnp.mean(dx * xhat, axis=-1, keepdims=True)
        out[...] = ((dx - m1 - xhat * m2) * rstd).astype(BF16)
    both = jnp.concatenate(projs + projs, axis=0)
    proj[...] = both.T[:, 0 : 2 * C]


def last_kernel(gwr, prs, gw, proj):
    gw[...] = jnp.sum(gwr[...].astype(F32), axis=0)
    proj[...] = jnp.sum(prs[...], axis=0)


def greet(n, me):
    barrier = pltpu.get_barrier_semaphore()
    for k in range(1, n):
        pl.semaphore_signal(
            barrier, inc=1, device_id={"col": lax.rem(me + k, n)},
            device_id_type=pl.DeviceIdType.MESH,
        )
    pl.semaphore_wait(barrier, n - 1)


def exchange_kernel(n, whole, count, *refs):
    ins, outs = refs[:count], refs[count : 2 * count]
    send, recv, own = refs[2 * count :]
    me = lax.axis_index("col")
    greet(n, me)
    copies = []
    for k in range(1, n):
        peer = lax.rem(me + k, n)
        for a in range(count):
            copy = pltpu.make_async_remote_copy(
                src_ref=ins[a] if whole[a] else ins[a].at[peer],
                dst_ref=outs[a].at[me],
                send_sem=send.at[a, k],
                recv_sem=recv.at[a, k],
                device_id={"col": peer},
                device_id_type=pl.DeviceIdType.MESH,
            )
            copy.start()
            copies.append(copy)
    for a in range(count):
        copy = pltpu.make_async_copy(
            ins[a] if whole[a] else ins[a].at[me], outs[a].at[me], own.at[a]
        )
        copy.start()
        copies.append(copy)
    for copy in copies:
        copy.wait()


def exchange(n, whole, cid, *arrays):
    count = len(arrays)
    return pl.pallas_call(
        functools.partial(exchange_kernel, n, whole, count),
        out_shape=[
            jax.ShapeDtypeStruct(((n,) + a.shape) if f else a.shape, a.dtype)
            for a, f in zip(arrays, whole)
        ],
        in_specs=[pl.BlockSpec(memory_space=pltpu.VMEM)] * count,
        out_specs=[pl.BlockSpec(memory_space=pltpu.VMEM)] * count,
        scratch_shapes=[
            pltpu.SemaphoreType.DMA((count, n)),
            pltpu.SemaphoreType.DMA((count, n)),
            pltpu.SemaphoreType.DMA((count,)),
        ],
        compiler_params=pltpu.CompilerParams(
            collective_id=cid, has_side_effects=True, vmem_limit_bytes=VMEM_LIMIT
        ),
        name="exchange%d" % cid,
    )(*arrays)


def call(kernel, outs, scratch, *args):
    return pl.pallas_call(
        kernel,
        out_shape=[jax.ShapeDtypeStruct(s, d) for s, d in outs],
        scratch_shapes=[pltpu.VMEM(s, d) for s, d in scratch],
        compiler_params=pltpu.CompilerParams(vmem_limit_bytes=VMEM_LIMIT),
    )(*args)


def per_device(n, xr, xc, sm, sc, cm, cc, gain, bias, wl, wr, w, pbias, g):
    lr = xr.shape[1]
    xr = xr.reshape(S * lr, M)
    xc = xc.reshape(S * J, M)
    sc, cc = sc[None, :], cc[None, :]
    gain, bias, pbias = gain[None, :], bias[None, :], pbias[None, :]
    g = g.reshape(NI * J, PW)
    cmt, wlt, wrt = cm.T, wl.T, wr.T
    halves = ((2, S * max(J, lr), 128), F32)
    left, right, gall, gy, gl = call(
        functools.partial(first_kernel, lr),
        [
            ((lr * H, 128), BF16), ((J * C, S), BF16), ((NI * J, PW), BF16),
            ((J * C, NI * C), BF16), ((NI * H, 128), BF16),
        ],
        [halves, ((NI * J, PW), F32), ((NI * H, 128), F32)],
        xr, xc, sm, sc, cmt, cc, gain, bias, wlt, wrt, g, w,
    )
    lic, glr = exchange(n, (True, False), 0, left, gl.reshape(n, lr * H, 128))
    pair, gw, grows, gcols, proj = call(
        functools.partial(middle_kernel, n, lr),
        [
            ((NI * J, PW), BF16), ((C * C, PW), BF16), ((S * lr, M), BF16), ((S * J, M), BF16),
            ((M, 2 * C), F32),
        ],
        [
            ((NI * H, 128), F32), ((NI * H, 128), BF16), ((C * C, NI * J), BF16),
            ((NI * J, PW), F32), halves, halves,
        ],
        lic.reshape(NI * H, 128), glr, right, gall, gy, w, pbias, xr, xc, sm, sc, cmt, cc,
        gain, bias, wlt, wrt,
    )
    gwr, prs = exchange(
        n, (False, False), 1, gw.reshape(n, C * C // n, PW), proj.reshape(n, M // n, 2 * C)
    )
    gw, proj = call(
        last_kernel, [((C * C // n, PW), F32), ((M // n, 2 * C), F32)], [], gwr, prs
    )
    return (
        pair.reshape(NI, J, PW),
        grows.reshape(S, lr, M),
        gcols.reshape(S, J, M),
        gw,
        proj,
    )


def solution(mesh):
    placed = (
        P("parts", "col", None), P("parts", "col", None), P("parts", None), P("parts"),
        P("parts", "col"), P(("parts", "col")), P(), P(), P(), P(), P(), P(),
        P("parts", "col", None),
    )
    return jax.shard_map(
        functools.partial(per_device, mesh.shape["col"]),
        mesh=mesh,
        in_specs=placed,
        out_specs=(
            P("parts", "col", None), P("parts", "col", None), P("parts", "col", None),
            P(("parts", "col"), None), P(("parts", "col"), None),
        ),
        check_vma=False,
    )
```

time: 122 us -> 73 us (0.60)
  Pallas kernels: 113 us -> 57.9 us
  local copies, waits for them, and re-layouts: 7.94 us -> 13.1 us
    pallas_call x3 -> x2, Pallas kernels: 97.5 us -> 40.8 us  [exchange(): pl.pallas_call(functools.partial(exchange_kernel, n, whole, count), out_s...]
    unnamed x37 -> x32, local copies, waits for them, and re-layouts: 7.94 us -> 13.1 us
    pallas_call x3, Pallas kernels: 15 us -> 17.1 us  [call(): pl.pallas_call(kernel, out_shape=[jax.ShapeDtypeStruct(s, d) for s, d in...]
where the time goes in v2:
time: 73 us; the launch traced here: 71.7 us
  Pallas kernels  57.9 us (79%)
  local copies, waits for them, and re-layouts  13.1 us (18%)
    pallas_call x2, Pallas kernels, exchange(): pl.pallas_call(functools.partial(exchange_kernel, n, whole, count), out_s...  40.8 us
    pallas_call x3, Pallas kernels, call(): pl.pallas_call(kernel, out_shape=[jax.ShapeDtypeStruct(s, d) for s, d in...  17.1 us
    unnamed x32, local copies, waits for them, and re-layouts  13.1 us

profile of v2, /device:TPU:0, one launch (start us, length us, event | category | flops | bytes accessed | tf_op | source)
XLA Modules:
  0.0 71.7 jit_solution(11848879793753405317)
XLA Ops:
  0.6 0.0 copy-start
  0.6 1.0 %copy-done = bf16[64,16,256]{2,1,0:T(8,128)(2,1)S(1)} copy-done((bf16[64,16,256]{2,1,0:T(8,128)(2,1)S(1)}, bf16[64,16,256]{2,1,0:T(8,128)(2,1)}, u32[]{:S(2)}) %copy-start) | copy-done | bytes 524312
  1.7 0.0 copy-start.2
  1.7 0.9 %copy-done.2 = bf16[64,8,256]{2,1,0:T(8,128)(2,1)S(1)} copy-done((bf16[64,8,256]{2,1,0:T(8,128)(2,1)S(1)}, bf16[64,8,256]{2,1,0:T(8,128)(2,1)}, u32[]{:S(2)}) %copy-start.2) | copy-done | bytes 262168
  2.6 0.0 copy-start.4
  2.6 0.9 %copy-done.4 = bf16[1024,128]{1,0:T(8,128)(2,1)S(1)} copy-done((bf16[1024,128]{1,0:T(8,128)(2,1)S(1)}, bf16[1024,128]{1,0:T(8,128)(2,1)}, u32[]{:S(2)}) %copy-start.4) | copy-done | bytes 262168
  3.6 0.0 copy-start.6
  3.6 1.0 %copy-done.6 = bf16[128,16,128]{2,1,0:T(8,128)(2,1)S(1)} copy-done((bf16[128,16,128]{2,1,0:T(8,128)(2,1)S(1)}, bf16[128,16,128]{2,1,0:T(8,128)(2,1)}, u32[]{:S(2)}) %copy-start.6) | copy-done | bytes 524312
  4.6 0.0 copy-start.7
  4.6 0.8 %copy-done.7 = s32[64,128]{1,0:T(8,128)S(1)} copy-done((s32[64,128]{1,0:T(8,128)S(1)}, s32[64,128]{1,0:T(8,128)}, u32[]{:S(2)}) %copy-start.7) | copy-done | bytes 32792
  5.4 0.0 copy-start.8
  5.4 0.7 copy-done.8
  6.1 0.0 copy-start.9
  6.1 0.7 copy-done.9
  6.8 0.0 copy-start.10
  6.8 0.7 copy-done.10
  7.5 0.0 copy-start.11
  7.5 0.7 copy-done.11
  8.2 0.0 copy-start.12
  8.2 0.7 copy-done.12
  8.9 0.0 copy-start.13
  8.9 0.7 copy-done.13
  9.5 0.0 copy-start.14
  9.5 0.7 copy-done.14
  10.2 4.4 %shard_map.164 = (bf16[128,128]{1,0:T(8,128)(2,1)S(1)}, bf16[512,64]{1,0:T(8,128)(2,1)S(1)}, bf16[2048,128]{1,0:T(8,128)(2,1)S(1)}, bf16[512,4096]{1,0:T(8,128)(2,1)}, bf16[2048,128]{1,0:T(8,128)(2,1)S(1)}) custom-call(bf16[512,256]{1,0:T(8,128)(2,1)S(1)} %bitcast.20, bf16[1024,256]{1,0:T(8,128)(2,1)S(1)} %bitcast.18, s32[64,128]{1,0:T(8,128)S(1)} %copy-done.7, ...), custom_call_target="tpu_custom_call" | custom-call | tf_op jit(solution)/shard_map/pallas_call | solution.py:248
  14.6 24.0 %exchange0.1 = (bf16[16,128,128]{2,1,0:T(8,128)(2,1)S(1)}, bf16[16,128,128]{2,1,0:T(8,128)(2,1)S(1)}) custom-call(bf16[128,128]{1,0:T(8,128)(2,1)S(1)} %get-tuple-element.21.refs_0_, bf16[16,128,128]{2,1,0:T(8,128)(2,1)S(1)} %bitcast.24), custom_call_target="tpu_custom_call" | custom-call | tf_op jit(solution)/shard_map/exchange0/pallas_call | solution.py:227
  38.6 0.0 copy-start.1
  38.7 1.0 %copy-done.1 = bf16[64,16,256]{2,1,0:T(8,128)(2,1)S(1)} copy-done((bf16[64,16,256]{2,1,0:T(8,128)(2,1)S(1)}, bf16[64,16,256]{2,1,0:T(8,128)(2,1)}, u32[]{:S(2)}) %copy-start.1) | copy-done | bytes 524312
  39.7 0.0 copy-start.3
  39.7 0.9 %copy-done.3 = bf16[64,8,256]{2,1,0:T(8,128)(2,1)S(1)} copy-done((bf16[64,8,256]{2,1,0:T(8,128)(2,1)S(1)}, bf16[64,8,256]{2,1,0:T(8,128)(2,1)}, u32[]{:S(2)}) %copy-start.3) | copy-done | bytes 262168
  40.6 0.0 copy-start.5
  40.6 0.9 %copy-done.5 = bf16[1024,128]{1,0:T(8,128)(2,1)S(1)} copy-done((bf16[1024,128]{1,0:T(8,128)(2,1)S(1)}, bf16[1024,128]{1,0:T(8,128)(2,1)}, u32[]{:S(2)}) %copy-start.5) | copy-done | bytes 262168
  41.6 0.0 copy-start.15
  41.6 0.7 copy-done.15
  42.2 12.0 %shard_map.165 = (bf16[2048,128]{1,0:T(8,128)(2,1)}, bf16[1024,128]{1,0:T(8,128)(2,1)S(1)}, bf16[512,256]{1,0:T(8,128)(2,1)}, bf16[1024,256]{1,0:T(8,128)(2,1)}, f32[256,64]{1,0:T(8,128)S(1)}) custom-call(bf16[2048,128]{1,0:T(8,128)(2,1)S(1)} %bitcast.22, bf16[16,128,128]{2,1,0:T(8,128)(2,1)S(1)} %get-tuple-element.24.glr, ...), custom_call_target="tpu_custom_call" | custom-call | tf_op jit(solution)/shard_map/pallas_call | solution.py:248
  54.2 16.8 %exchange1.1 = (bf16[16,64,128]{2,1,0:T(8,128)(2,1)S(1)}, f32[16,16,64]{2,1,0:T(8,128)S(1)}) custom-call(bf16[16,64,128]{2,1,0:T(8,128)(2,1)S(1)} %bitcast.25, f32[16,16,64]{2,1,0:T(8,128)S(1)} %bitcast.26), custom_call_target="tpu_custom_call" | custom-call | tf_op jit(solution)/shard_map/exchange1/pallas_call | solution.py:227
  71.0 0.7 shard_map.166
Async XLA Ops:
  0.6 1.0 %copy-start = (bf16[64,16,256]{2,1,0:T(8,128)(2,1)S(1)}, bf16[64,16,256]{2,1,0:T(8,128)(2,1)}, u32[]{:S(2)}) copy-start(bf16[64,16,256]{2,1,0:T(8,128)(2,1)} %param.14) | copy-start | bytes 1572868
  1.7 0.9 %copy-start.2 = (bf16[64,8,256]{2,1,0:T(8,128)(2,1)S(1)}, bf16[64,8,256]{2,1,0:T(8,128)(2,1)}, u32[]{:S(2)}) copy-start(bf16[64,8,256]{2,1,0:T(8,128)(2,1)} %param.13) | copy-start | bytes 786436
  2.6 0.9 %copy-start.4 = (bf16[1024,128]{1,0:T(8,128)(2,1)S(1)}, bf16[1024,128]{1,0:T(8,128)(2,1)}, u32[]{:S(2)}) copy-start(bf16[1024,128]{1,0:T(8,128)(2,1)} %w.3) | copy-start | bytes 786436
  3.6 1.0 %copy-start.6 = (bf16[128,16,128]{2,1,0:T(8,128)(2,1)S(1)}, bf16[128,16,128]{2,1,0:T(8,128)(2,1)}, u32[]{:S(2)}) copy-start(bf16[128,16,128]{2,1,0:T(8,128)(2,1)} %param.25) | copy-start | bytes 1572868
  4.6 0.8 %copy-start.7 = (s32[64,128]{1,0:T(8,128)S(1)}, s32[64,128]{1,0:T(8,128)}, u32[]{:S(2)}) copy-start(s32[64,128]{1,0:T(8,128)} %sm.3) | copy-start | bytes 98308
  5.4 0.7 %copy-start.8 = (bf16[256,32]{0,1:T(8,128)(2,1)S(1)}, bf16[256,32]{0,1:T(8,128)(2,1)}, u32[]{:S(2)}) copy-start(bf16[256,32]{0,1:T(8,128)(2,1)} %param.21) | copy-start | bytes 49156
  6.1 0.7 %copy-start.9 = (bf16[256,32]{0,1:T(8,128)(2,1)S(1)}, bf16[256,32]{0,1:T(8,128)(2,1)}, u32[]{:S(2)}) copy-start(bf16[256,32]{0,1:T(8,128)(2,1)} %param.22) | copy-start | bytes 49156
  6.8 0.7 copy-start.10
  7.5 0.7 copy-start.11
  8.2 0.7 copy-start.12
  8.9 0.7 copy-start.13
  9.5 0.7 copy-start.14
  38.6 1.0 %copy-start.1 = (bf16[64,16,256]{2,1,0:T(8,128)(2,1)S(1)}, bf16[64,16,256]{2,1,0:T(8,128)(2,1)}, u32[]{:S(2)}) copy-start(bf16[64,16,256]{2,1,0:T(8,128)(2,1)} %param.14) | copy-start | bytes 1572868
  39.7 0.9 %copy-start.3 = (bf16[64,8,256]{2,1,0:T(8,128)(2,1)S(1)}, bf16[64,8,256]{2,1,0:T(8,128)(2,1)}, u32[]{:S(2)}) copy-start(bf16[64,8,256]{2,1,0:T(8,128)(2,1)} %param.13) | copy-start | bytes 786436
  40.6 0.9 %copy-start.5 = (bf16[1024,128]{1,0:T(8,128)(2,1)S(1)}, bf16[1024,128]{1,0:T(8,128)(2,1)}, u32[]{:S(2)}) copy-start(bf16[1024,128]{1,0:T(8,128)(2,1)} %w.3) | copy-start | bytes 786436
  41.6 0.7 copy-start.15

commit v3 on v1

v3 whole, which is shorter than its diff:
```python
import functools

import jax
import jax.numpy as jnp
from jax import lax
from jax.experimental import pallas as pl
from jax.experimental.pallas import tpu as pltpu
from jax.sharding import PartitionSpec as P

F32 = jnp.float32
BF16 = jnp.bfloat16
M = 256
C = 32
H = C // 2
PW = 128
S = 64
NI = 128
J = 16
EPS = 1e-05
VMEM_LIMIT = 63 * 1024 * 1024

NN = (((1,), (0,)), ((), ()))
NT = (((1,), (1,)), ((), ()))
TN = (((0,), (0,)), ((), ()))


def dot(a, b, dims=NN):
    return lax.dot_general(a, b, dims, preferred_element_type=F32)


def eye(n):
    r = lax.broadcasted_iota(jnp.int32, (n, n), 0)
    c = lax.broadcasted_iota(jnp.int32, (n, n), 1)
    return (r == c).astype(F32).astype(BF16)


def turned(a):
    return dot(eye(a.shape[1]), a, NT)


def row_weights(sm_ref, sc_ref):
    return (sm_ref[...] * sc_ref[...]).astype(F32).astype(BF16)


def col_weights_t(cmt_ref, cc_ref):
    crop = jnp.broadcast_to(cc_ref[...].astype(F32), (8, J)).astype(BF16)
    return cmt_ref[...].astype(F32) * turned(crop)[:, 0:1]


def local_weights_t(rw, lr):
    pad = max(lr, 8)
    first = lax.axis_index("col") * lr
    r = lax.broadcasted_iota(jnp.int32, (pad, NI), 0) + first
    c = lax.broadcasted_iota(jnp.int32, (pad, NI), 1)
    return dot((r == c).astype(F32).astype(BF16), rw, NT)


def normalize(x):
    mean = jnp.mean(x, axis=-1, keepdims=True)
    center = x - mean
    rstd = lax.rsqrt(jnp.mean(center * center, axis=-1, keepdims=True) + EPS)
    return center * rstd, rstd


def put_halves(ref, rows, value):
    ref[0, 0:rows, :] = value[:, 0:128]
    ref[1, 0:rows, :] = value[:, 128:256]


def get_halves(ref, start, stride):
    return jnp.concatenate(
        [ref[h, pl.ds(start, S, stride), :] for h in range(2)], axis=1
    )


def inverse_denom(cw, rw):
    return 1.0 / jnp.maximum(dot(cw.astype(BF16), rw), 1.0)


def lanes(ref, i, j):
    return jnp.concatenate([ref[i], ref[j]], axis=1)


def body(n, lr, *refs):
    hbm, refs = refs[:COUNT], refs[COUNT:]
    (pair, grows, gcols, gw, proj), refs = refs[:5], refs[5:]
    ins, refs = refs[:COUNT], refs[COUNT:]
    (
        left, lic, gls, glr, gws, gwr, prs, prr, right, gall, gy, o, lt, l32, g32, gl32, p32,
        bufr, bufc, xhr, xhc, rsr, rsc, dbr, dbc, in_sem, send, recv,
    ) = refs
    xr, xc, sm, sc, cmt, cc, gain, bias, wlt, wrt, w, pbias, g = ins
    me = lax.axis_index("col")
    barrier = pltpu.get_barrier_semaphore()
    for k in range(1, n):
        pl.semaphore_signal(
            barrier, inc=1, device_id={"col": lax.rem(me + k, n)},
            device_id_type=pl.DeviceIdType.MESH,
        )
    loads = [pltpu.make_async_copy(hbm[i], ins[i], in_sem.at[i]) for i in range(COUNT)]
    for copy in loads:
        copy.start()

    def exchange(a, src, dst, whole):
        copies = []
        for k in range(1, n):
            peer = lax.rem(me + k, n)
            copy = pltpu.make_async_remote_copy(
                src_ref=src if whole else src.at[peer],
                dst_ref=dst.at[me],
                send_sem=send.at[a, k],
                recv_sem=recv.at[a, k],
                device_id={"col": peer},
                device_id_type=pl.DeviceIdType.MESH,
            )
            copy.start()
            copies.append(copy)
        dst[me] = src[...] if whole else src[me]
        return copies

    for i in (2, 3, 4, 5, 6, 7, 8, 9, 0):
        loads[i].wait()
    rw = row_weights(sm, sc)
    lw = local_weights_t(rw, lr)
    cw = col_weights_t(cmt, cc)
    inv = inverse_denom(cw, rw)

    def norm(x_ref, count, xh, rs, buf):
        xhat, rstd = normalize(x_ref[...].astype(F32))
        xh[...] = xhat
        rs[...] = rstd
        normed = (xhat * gain[...] + bias[...]).astype(BF16)
        put_halves(buf, S * count, normed.astype(F32))

    norm(xr, lr, xhr, rsr, bufr)
    for i in range(lr):
        prod = dot(wlt[...], get_halves(bufr, i, lr).astype(BF16), NT) * lw[i : i + 1, :]
        left[i * H : (i + 1) * H, :] = jnp.concatenate(
            [prod[0:H, :], prod[H:C, :]], axis=1
        ).astype(BF16)
    pl.semaphore_wait(barrier, n - 1)
    gather = exchange(0, left, lic, True)

    loads[1].wait()
    norm(xc, J, xhc, rsc, bufc)
    for j in range(J):
        prod = dot(wrt[...], get_halves(bufc, j, J).astype(BF16), NT)
        right[j * C : (j + 1) * C, :] = (prod * cw[j : j + 1, :]).astype(BF16)
    for i in (10, 11, 12):
        loads[i].wait()
    g32[...] = g[...].astype(F32)
    wv = w[...]
    for j in range(J):
        gj = g32[pl.ds(j, NI, J), :].astype(BF16)
        gall[j * NI : (j + 1) * NI, :] = gj
        go = (dot(wv, gj, NT) * inv[j : j + 1, :]).astype(BF16)
        gy[:, j * C : (j + 1) * C, :] = go.reshape(C, C, NI)
    rt = right[...]
    r = turned(rt).astype(BF16)
    for c in range(H):
        both = jnp.concatenate([dot(r, gy[c]), dot(r, gy[c + H])], axis=0)
        gl32[pl.ds(c, NI, H), :] = both.T
    gls[...] = gl32[...].astype(BF16).reshape(n, lr * H, 128)
    lefts = exchange(1, gls, glr, False)

    for copy in gather:
        copy.wait_recv()
    l32[...] = lic[...].astype(F32).reshape(NI * H, 128)
    zero = jnp.zeros_like(rt)
    rts = (jnp.concatenate([rt, zero], axis=1), jnp.concatenate([zero, rt], axis=1))
    inv3 = inv[:, None, :]
    for c in range(H):
        lc = l32[pl.ds(c, NI, H), :].astype(BF16)
        lt[c * NI : (c + 1) * NI, :] = lc
        for h in range(2):
            y = dot(rts[h], lc, NT)
            at = (h * H + c) * C
            o[:, at : at + C, :] = (y.reshape(J, C, NI) * inv3).astype(BF16)
    acc = jnp.zeros((C * C, PW), F32)
    for j in range(0, J, 2):
        acc = acc + dot(lanes(o, j, j + 1), gall[j * NI : (j + 2) * NI, :])
    gws[...] = acc.astype(BF16).reshape(n, C * C // n, PW)
    weights = exchange(2, gws, gwr, False)

    halves = []
    for h in range(2):
        acc = jnp.zeros((J * C, 2 * S), F32)
        for c in range(0, H, 2):
            acc = acc + dot(lanes(gy, h * H + c, h * H + c + 1), lt[c * NI : (c + 2) * NI, :])
        halves.append(acc[:, h * S : (h + 1) * S])
    racc = halves[0] + halves[1]

    def back(count, grad, weights_t, buf, w_ref, db):
        ptot = jnp.zeros((C, M), F32)
        for i in range(count):
            gi = (grad(i) * weights_t[i : i + 1, :]).astype(BF16)
            ptot = ptot + dot(gi, get_halves(buf, i, count).astype(BF16))
            dn = dot(turned(gi).astype(BF16), w_ref[...])
            db[0, pl.ds(i, S, count), :] = dn[:, 0:128]
            db[1, pl.ds(i, S, count), :] = dn[:, 128:256]
        return ptot

    def norm_back(out, db, xh, rs):
        dx = jnp.concatenate([db[0], db[1]], axis=1) * gain[...]
        xhat = xh[...]
        m1 = jnp.mean(dx, axis=-1, keepdims=True)
        m2 = jnp.mean(dx * xhat, axis=-1, keepdims=True)
        out[...] = ((dx - m1 - xhat * m2) * rs[...]).astype(BF16)

    pright = back(J, lambda i: racc[i * C : (i + 1) * C, :], cw, bufc, wrt, dbc)
    for copy in lefts:
        copy.wait_recv()
    total = jnp.sum(glr[...].astype(F32), axis=0)

    def left_grad(i):
        ti = total[i * H : (i + 1) * H, :]
        return jnp.concatenate([ti[:, 0:S], ti[:, S : 2 * S]], axis=0)

    pleft = back(lr, left_grad, lw, bufr, wlt, dbr)
    stacked = jnp.concatenate([pleft, pright, pleft, pright], axis=0)
    prs[...] = stacked.T[:, 0 : 2 * C].reshape(n, M // n, 2 * C)
    projs = exchange(3, prs, prr, False)

    for j in range(J):
        p32[pl.ds(j, NI, J), :] = dot(o[j], wv, TN) + pbias[...]
    pair[...] = p32[...].astype(BF16)
    norm_back(grows, dbr, xhr, rsr)
    norm_back(gcols, dbc, xhc, rsc)
    for copy in weights:
        copy.wait_recv()
    gw[...] = jnp.sum(gwr[...].astype(F32), axis=0)
    for copy in projs:
        copy.wait_recv()
    proj[...] = jnp.sum(prr[...], axis=0)
    for copy in gather + lefts + weights + projs:
        copy.wait_send()


COUNT = 13


def per_device(n, xr, xc, sm, sc, cm, cc, gain, bias, wl, wr, w, pbias, g):
    lr = xr.shape[1]
    args = (
        xr.reshape(S * lr, M), xc.reshape(S * J, M), sm, sc[None, :], cm.T, cc[None, :],
        gain[None, :], bias[None, :], wl.T, wr.T, w, pbias[None, :], g.reshape(NI * J, PW),
    )
    vmem = pltpu.VMEM
    part = C * C // n
    pair, grows, gcols, gw, proj = pl.pallas_call(
        functools.partial(body, n, lr),
        out_shape=[
            jax.ShapeDtypeStruct((NI * J, PW), BF16),
            jax.ShapeDtypeStruct((S * lr, M), BF16),
            jax.ShapeDtypeStruct((S * J, M), BF16),
            jax.ShapeDtypeStruct((part, PW), F32),
            jax.ShapeDtypeStruct((M // n, 2 * C), F32),
        ],
        in_specs=[pl.BlockSpec(memory_space=pltpu.HBM)] * COUNT,
        out_specs=[pl.BlockSpec(memory_space=pltpu.VMEM)] * 5,
        scratch_shapes=[vmem(a.shape, a.dtype) for a in args]
        + [
            vmem((lr * H, 128), BF16), vmem((n, lr * H, 128), BF16),
            vmem((n, lr * H, 128), BF16), vmem((n, lr * H, 128), BF16),
            vmem((n, part, PW), BF16), vmem((n, part, PW), BF16),
            vmem((n, M // n, 2 * C), F32), vmem((n, M // n, 2 * C), F32),
            vmem((J * C, S), BF16), vmem((NI * J, PW), BF16),
            vmem((C, J * C, NI), BF16), vmem((J, C * C, NI), BF16), vmem((NI * H, 128), BF16),
            vmem((NI * H, 128), F32), vmem((NI * J, PW), F32), vmem((NI * H, 128), F32),
            vmem((NI * J, PW), F32),
            vmem((2, S * lr, 128), F32), vmem((2, S * J, 128), F32),
            vmem((S * lr, M), F32), vmem((S * J, M), F32),
            vmem((S * lr, 1), F32), vmem((S * J, 1), F32),
            vmem((2, S * lr, 128), F32), vmem((2, S * J, 128), F32),
            pltpu.SemaphoreType.DMA((COUNT,)),
            pltpu.SemaphoreType.DMA((4, n)), pltpu.SemaphoreType.DMA((4, n)),
        ],
        compiler_params=pltpu.CompilerParams(
            collective_id=0, has_side_effects=True, vmem_limit_bytes=VMEM_LIMIT
        ),
        name="outer_product_mean",
    )(*args)
    return (
        pair.reshape(NI, J, PW),
        grows.reshape(S, lr, M),
        gcols.reshape(S, J, M),
        gw,
        proj,
    )


def solution(mesh):
    placed = (
        P("parts", "col", None), P("parts", "col", None), P("parts", None), P("parts"),
        P("parts", "col"), P(("parts", "col")), P(), P(), P(), P(), P(), P(),
        P("parts", "col", None),
    )
    return jax.shard_map(
        functools.partial(per_device, mesh.shape["col"]),
        mesh=mesh,
        in_specs=placed,
        out_specs=(
            P("parts", "col", None), P("parts", "col", None), P("parts", "col", None),
            P(("parts", "col"), None), P(("parts", "col"), None),
        ),
        check_vma=False,
    )
```

time: 122 us -> 47.9 us (0.39)
  Pallas kernels: 113 us -> 42.3 us
  local copies, waits for them, and re-layouts: 7.94 us -> 4.75 us
    pallas_call x6 -> x1, Pallas kernels: 113 us -> 42.3 us  [per_device(): pl.pallas_call(functools.partial(body, n, lr), out_shape=[jax.ShapeDtypeS...]
    unnamed x37 -> x13, local copies, waits for them, and re-layouts: 7.94 us -> 4.75 us
where the time goes in v3:
time: 47.9 us; the launch traced here: 47.7 us
  Pallas kernels  42.3 us (88%)
  local copies, waits for them, and re-layouts  4.75 us (10%)
  between operations  0.67 us (1%)
    pallas_call x1, Pallas kernels, per_device(): pl.pallas_call(functools.partial(body, n, lr), out_shape=[jax.ShapeDtypeS...  42.3 us
    unnamed x13, local copies, waits for them, and re-layouts  4.75 us

profile of v3, /device:TPU:0, one launch (start us, length us, event | category | flops | bytes accessed | tf_op | source)
XLA Modules:
  0.0 47.7 jit_solution(3229280577047160322)
XLA Ops:
  0.6 42.3 %outer_product_mean.1 = (bf16[2048,128]{1,0:T(8,128)(2,1)}, bf16[512,256]{1,0:T(8,128)(2,1)}, bf16[1024,256]{1,0:T(8,128)(2,1)}, f32[64,128]{1,0:T(8,128)}, f32[16,64]{1,0:T(8,128)}) custom-call(bf16[512,256]{1,0:T(8,128)(2,1)} %bitcast.19, bf16[1024,256]{1,0:T(8,128)(2,1)} %bitcast.16, s32[64,128]{1,0:T(8,128)} %refs_2_.1, s32[1,128]{1,0:T(1,128)} %bitcast.25, ...), custom_call_target="tpu_custom_call" | custom-call | tf_op jit(solution)/shard_map/outer_product_mean/pallas_call | solution.py:250
  42.9 0.0 copy-start.1
  42.9 0.0 copy-start
  42.9 1.9 %copy.23 = bf16[128,16,128]{2,1,0:T(8,128)(2,1)} copy(bf16[128,16,128]{2,1,0:T(8,128)(2,1)} %bitcast.15) | data formatting | bytes 1048576
  44.9 0.0 copy-done.1
  44.9 0.7 %copy.24 = bf16[64,8,256]{2,1,0:T(8,128)(2,1)} copy(bf16[64,8,256]{2,1,0:T(8,128)(2,1)S(1)} %bitcast.18) | data formatting | bytes 524288
  45.6 0.0 copy-done
  45.6 0.0 copy-start.2
  45.6 0.8 %copy.25 = bf16[64,16,256]{2,1,0:T(8,128)(2,1)} copy(bf16[64,16,256]{2,1,0:T(8,128)(2,1)S(1)} %bitcast.14) | data formatting | bytes 1048576
  46.4 0.0 copy-done.2
  46.4 0.0 copy-start.3
  46.4 0.6 %copy.26 = f32[64,128]{1,0:T(8,128)} copy(f32[64,128]{1,0:T(8,128)S(1)} %copy-done.2) | data formatting | bytes 65536
  47.0 0.1 copy-done.3
  47.1 0.6 %copy.27 = f32[16,64]{1,0:T(8,128)} copy(f32[16,64]{1,0:T(8,128)S(1)} %copy-done.3) | data formatting | bytes 8192
Async XLA Ops:
  42.9 2.0 %copy-start.1 = (bf16[512,256]{1,0:T(8,128)(2,1)S(1)}, bf16[512,256]{1,0:T(8,128)(2,1)}, u32[]{:S(2)}) copy-start(bf16[512,256]{1,0:T(8,128)(2,1)} %get-tuple-element.11) | copy-start | bytes 786436
  42.9 2.7 %copy-start = (bf16[1024,256]{1,0:T(8,128)(2,1)S(1)}, bf16[1024,256]{1,0:T(8,128)(2,1)}, u32[]{:S(2)}) copy-start(bf16[1024,256]{1,0:T(8,128)(2,1)} %get-tuple-element.12) | copy-start | bytes 1572868
  45.6 0.8 %copy-start.2 = (f32[64,128]{1,0:T(8,128)S(1)}, f32[64,128]{1,0:T(8,128)}, u32[]{:S(2)}) copy-start(f32[64,128]{1,0:T(8,128)} %get-tuple-element.23) | copy-start | bytes 98308
  46.4 0.7 %copy-start.3 = (f32[16,64]{1,0:T(8,128)S(1)}, f32[16,64]{1,0:T(8,128)}, u32[]{:S(2)}) copy-start(f32[16,64]{1,0:T(8,128)} %get-tuple-element.24) | copy-start | bytes 12292

commit v4 on v3

--- a/solution.py
+++ b/solution.py
@@ -139,7 +139,24 @@
             [prod[0:H, :], prod[H:C, :]], axis=1
         ).astype(BF16)
     pl.semaphore_wait(barrier, n - 1)
-    gather = exchange(0, left, lic, True)
+    half = n // 2
+    other = me + 1 - 2 * lax.rem(me, 2)
+
+    def pass_on(k, src, at, peer):
+        copy = pltpu.make_async_remote_copy(
+            src_ref=src,
+            dst_ref=lic.at[at],
+            send_sem=send.at[0, k],
+            recv_sem=recv.at[0, k],
+            device_id={"col": peer},
+            device_id_type=pl.DeviceIdType.MESH,
+        )
+        copy.start()
+        return copy
+
+    direct = [pass_on(k, left, me, lax.rem(me + 2 * k, n)) for k in range(1, half)]
+    gather = [pass_on(0, left, me, other)]
+    lic[me] = left[...]
 
     loads[1].wait()
     norm(xc, J, xhc, rsc, bufc)
@@ -163,6 +180,10 @@
     gls[...] = gl32[...].astype(BF16).reshape(n, lr * H, 128)
     lefts = exchange(1, gls, glr, False)
 
+    for k in range(1, half):
+        direct[k - 1].wait_recv()
+        at = lax.rem(me - 2 * k + n, n)
+        gather.append(pass_on(half + k, lic.at[at], at, other))
     for copy in gather:
         copy.wait_recv()
     l32[...] = lic[...].astype(F32).reshape(NI * H, 128)
@@ -232,7 +253,7 @@
     for copy in projs:
         copy.wait_recv()
     proj[...] = jnp.sum(prr[...], axis=0)
-    for copy in gather + lefts + weights + projs:
+    for copy in direct + gather + lefts + weights + projs:
         copy.wait_send()
 
 

time: 47.9 us -> 42.5 us (0.89)
  Pallas kernels: 42.3 us -> 36.8 us
    pallas_call x1, Pallas kernels: 42.3 us -> 36.8 us  [per_device(): pl.pallas_call(functools.partial(body, n, lr), out_shape=[jax.ShapeDtypeS...]
where the time goes in v4:
time: 42.5 us; the launch traced here: 42.2 us
  Pallas kernels  36.8 us (87%)
  local copies, waits for them, and re-layouts  4.75 us (11%)
  between operations  0.67 us (2%)
    pallas_call x1, Pallas kernels, per_device(): pl.pallas_call(functools.partial(body, n, lr), out_shape=[jax.ShapeDtypeS...  36.8 us
    unnamed x13, local copies, waits for them, and re-layouts  4.75 us

profile of v4, /device:TPU:0, one launch (start us, length us, event | category | flops | bytes accessed | tf_op | source)
XLA Modules:
  0.0 42.2 jit_solution(10593385443070533198)
XLA Ops:
  0.6 36.8 %outer_product_mean.1 = (bf16[2048,128]{1,0:T(8,128)(2,1)}, bf16[512,256]{1,0:T(8,128)(2,1)}, bf16[1024,256]{1,0:T(8,128)(2,1)}, f32[64,128]{1,0:T(8,128)}, f32[16,64]{1,0:T(8,128)}) custom-call(bf16[512,256]{1,0:T(8,128)(2,1)} %bitcast.19, bf16[1024,256]{1,0:T(8,128)(2,1)} %bitcast.16, s32[64,128]{1,0:T(8,128)} %refs_2_.1, s32[1,128]{1,0:T(1,128)} %bitcast.25, ...), custom_call_target="tpu_custom_call" | custom-call | tf_op jit(solution)/shard_map/outer_product_mean/pallas_call | solution.py:271
  37.5 0.0 copy-start.1
  37.5 0.0 copy-start
  37.5 1.9 %copy.23 = bf16[128,16,128]{2,1,0:T(8,128)(2,1)} copy(bf16[128,16,128]{2,1,0:T(8,128)(2,1)} %bitcast.15) | data formatting | bytes 1048576
  39.4 0.0 copy-done.1
  39.4 0.7 %copy.24 = bf16[64,8,256]{2,1,0:T(8,128)(2,1)} copy(bf16[64,8,256]{2,1,0:T(8,128)(2,1)S(1)} %bitcast.18) | data formatting | bytes 524288
  40.1 0.0 copy-done
  40.1 0.0 copy-start.2
  40.1 0.8 %copy.25 = bf16[64,16,256]{2,1,0:T(8,128)(2,1)} copy(bf16[64,16,256]{2,1,0:T(8,128)(2,1)S(1)} %bitcast.14) | data formatting | bytes 1048576
  40.9 0.0 copy-done.2
  40.9 0.0 copy-start.3
  40.9 0.6 %copy.26 = f32[64,128]{1,0:T(8,128)} copy(f32[64,128]{1,0:T(8,128)S(1)} %copy-done.2) | data formatting | bytes 65536
  41.6 0.1 copy-done.3
  41.6 0.6 %copy.27 = f32[16,64]{1,0:T(8,128)} copy(f32[16,64]{1,0:T(8,128)S(1)} %copy-done.3) | data formatting | bytes 8192
Async XLA Ops:
  37.5 2.0 %copy-start.1 = (bf16[512,256]{1,0:T(8,128)(2,1)S(1)}, bf16[512,256]{1,0:T(8,128)(2,1)}, u32[]{:S(2)}) copy-start(bf16[512,256]{1,0:T(8,128)(2,1)} %get-tuple-element.11) | copy-start | bytes 786436
  37.5 2.7 %copy-start = (bf16[1024,256]{1,0:T(8,128)(2,1)S(1)}, bf16[1024,256]{1,0:T(8,128)(2,1)}, u32[]{:S(2)}) copy-start(bf16[1024,256]{1,0:T(8,128)(2,1)} %get-tuple-element.12) | copy-start | bytes 1572868
  40.1 0.8 %copy-start.2 = (f32[64,128]{1,0:T(8,128)S(1)}, f32[64,128]{1,0:T(8,128)}, u32[]{:S(2)}) copy-start(f32[64,128]{1,0:T(8,128)} %get-tuple-element.23) | copy-start | bytes 98308
  40.9 0.7 %copy-start.3 = (f32[16,64]{1,0:T(8,128)S(1)}, f32[16,64]{1,0:T(8,128)}, u32[]{:S(2)}) copy-start(f32[16,64]{1,0:T(8,128)} %get-tuple-element.24) | copy-start | bytes 12292
